TPU v7x, 32 devices: a whole 2x2x4 slice. The times are simulated.
32 devices in a mesh: expert: 8 (over y, x, core), dp: 4 (over z).
Axes of the slice: x: 2, y: 2, z: 4, core: 2. Of those that a mesh axis runs over, the one named last changes fastest.
Arguments:
- trunk: bfloat16 [768, 4096], P(('dp', 'expert')), may hold values from -6 to 6
- w_first: bfloat16 [8, 4096, 2048], P('expert'), may hold values from -0.09375 to 0.09375
- w_second: bfloat16 [8, 2048, 1024], P('expert'), may hold values from -0.125 to 0.125
- gates: bfloat16 [8, 8, 768], P('expert', None, 'dp'), may hold values from 0.049804688 to 1
- d_mixed: bfloat16 [768, 8, 1024], P(('dp', 'expert')), may hold values from -6 to 6
Outputs:
- mixed: bfloat16 [768, 8, 1024], P(('dp', 'expert'))
- d_trunk: bfloat16 [768, 4096], P(('dp', 'expert'))
- d_gates: bfloat16 [8, 8, 768], P('expert', None, 'dp')
- d_w_first: bfloat16 [8, 4096, 2048], P('expert', 'dp')
- d_w_second: bfloat16 [8, 2048, 1024], P('expert', 'dp')
All inputs are finite; a program needn't handle non-finite values.
Results may differ from a plain program's by a relative error of at most 0.015.
Values may be sent and summed in bfloat16 or wider, within the bound.
A program may use at most 128 MiB of HBM per device.

v0:
```python
import functools

import jax
import jax.numpy as jnp
from jax import lax
from jax.experimental import pallas as pl
from jax.experimental.pallas import tpu as pltpu
from jax.sharding import PartitionSpec as P

F32 = jnp.float32
BF16 = jnp.bfloat16


MESH = pl.DeviceIdType.MESH


def gather_kernel(n_e, n_d, trunk, gates, cot, first, second, rows, d_out, pre, gate_each,
                  outs, weights, later, hidden, made, m_send, m_recv, later_sem, piece, block, tall, w_sem, load_sem, store_sem,
                  g_send, g_recv, t_send, t_recv, o_send, o_recv, z_send, z_recv,
                  own_sem):
    e = lax.axis_index("expert")
    z = lax.axis_index("dp")
    partner = e + 1 - 2 * lax.rem(e, 2)
    pairs = n_e // 2

    def plane(s):
        return lax.rem(e + s, n_e)

    def along(i):
        return lax.rem(z + i, n_d)

    def remote(src, dst, send, recv, where):
        return pltpu.make_async_remote_copy(
            src_ref=src, dst_ref=dst, send_sem=send, recv_sem=recv,
            device_id=where, device_id_type=MESH)

    load_weights = pltpu.make_async_copy(first, weights, w_sem)
    load_weights.start()
    load_later = pltpu.make_async_copy(second, later, later_sem)
    load_later.start()

    barrier = pltpu.get_barrier_semaphore()
    for s in range(1, n_e):
        pl.semaphore_signal(barrier, inc=1, device_id={"expert": plane(s)}, device_id_type=MESH)
    for i in range(1, n_d):
        pl.semaphore_signal(barrier, inc=1, device_id={"dp": along(i)}, device_id_type=MESH)
    pl.semaphore_wait(barrier, n_e - 1 + n_d - 1)

    sent = []

    def go(copy):
        copy.start()
        sent.append(copy)

    for s in range(1, n_e):
        j = plane(s)
        go(remote(gates.at[j], gate_each.at[e], g_send.at[s], g_recv.at[e], {"expert": j}))
    own_gate = pltpu.make_async_copy(gates.at[e], gate_each.at[e], own_sem.at[0])
    own_gate.start()
    own_rows = pltpu.make_async_copy(trunk, rows.at[z, e], own_sem.at[1])
    own_rows.start()

    def spread(i):
        zi = along(i)
        src = trunk if i == 0 else rows.at[zi, e]
        for s in range(1, pairs):
            go(remote(src, rows.at[zi, e], t_send.at[i, s], t_recv.at[zi, e],
                      {"expert": plane(2 * s)}))
        go(remote(src, rows.at[zi, e], t_send.at[i, 0], t_recv.at[zi, e], {"expert": partner}))

    def arrived(zi, j):
        remote(trunk, rows.at[zi, j], t_send.at[0, 0], t_recv.at[zi, j],
               {"expert": partner}).wait_recv()

    for i in range(1, n_d):
        go(remote(trunk, rows.at[z, e], t_send.at[i, n_e - 1], t_recv.at[z, e], {"dp": along(i)}))
    spread(0)

    for s in range(1, n_e):
        j = plane(s)
        remote(gates.at[j], gate_each.at[j], g_send.at[0], g_recv.at[j], {"expert": j}).wait_recv()
    own_gate.wait()
    tasks = cot.shape[0]

    @pl.loop(0, n_e)
    def _(j):
        weight = gate_each[j]
        total = weight[:, 0:1] * cot[0].astype(F32)
        for t in range(1, tasks):
            total = total + weight[:, t:t + 1] * cot[t].astype(F32)
        piece[j] = total.astype(BF16)

    own_piece = pltpu.make_async_copy(piece.at[e], d_out.at[z, e], own_sem.at[2])
    own_piece.start()
    for s in range(1, n_e):
        j = plane(s)
        go(remote(piece.at[j], d_out.at[z, e], o_send.at[s], o_recv.at[e], {"expert": j}))

    def send_outputs():
        own_made.start()
        for s in range(1, n_e):
            j = plane(s)
            go(remote(made.at[j], outs.at[e], m_send.at[s], m_recv.at[e], {"expert": j}))

    own_made = pltpu.make_async_copy(made.at[e], outs.at[e], own_sem.at[3])
    stores = []
    for i in range(n_d):
        zi = along(i)
        if i + 1 < n_d:
            arrived(along(i + 1), e)
            spread(i + 1)
        if i == 1:
            send_outputs()
        if i == 0:
            for s in range(1, n_e):
                j = plane(s)
                remote(piece.at[j], d_out.at[z, j], o_send.at[0], o_recv.at[j],
                       {"expert": j}).wait_recv()
            own_piece.wait()
            for k in range(1, n_d):
                go(remote(d_out.at[z], d_out.at[z], z_send.at[k], z_recv.at[z], {"dp": along(k)}))
            own_rows.wait()
        for s in range(1, pairs):
            j = plane(2 * s)
            arrived(zi, j)
            go(remote(rows.at[zi, j], rows.at[zi, j], t_send.at[i, pairs - 1 + s],
                      t_recv.at[zi, j], {"expert": partner}))
        for s in range(pairs):
            arrived(zi, lax.rem(partner + 2 * s, n_e))
        load = pltpu.make_async_copy(rows.at[zi], block, load_sem)
        load.start()
        if i == 0:
            load_weights.wait()
        else:
            stores[-1].wait()
        load.wait()
        height = block.shape[0] * block.shape[1]
        tile = 256
        left = block[...].reshape(height, block.shape[2])

        @pl.loop(0, tall.shape[1] // tile)
        def _(c):
            here = pl.ds(pl.multiple_of(c * tile, tile), tile)
            value = jnp.dot(left, weights[:, here], preferred_element_type=F32)
            tall[:, here] = value
            if i == 0:
                hidden[:, here] = (value * jax.nn.sigmoid(value)).astype(BF16)

        store = pltpu.make_async_copy(tall, pre.at[zi], store_sem)
        store.start()
        stores.append(store)
        if i == 0:
            load_later.wait()

            @pl.loop(0, made.shape[2] // tile)
            def _(c):
                here = pl.ds(pl.multiple_of(c * tile, tile), tile)
                value = jnp.dot(hidden[...], later[:, here], preferred_element_type=F32)
                made[:, :, here] = value.astype(BF16).reshape(n_e, -1, tile)

    stores[-1].wait()
    if n_d == 1:
        send_outputs()
    own_made.wait()
    for s in range(1, n_e):
        j = plane(s)
        remote(made.at[j], outs.at[j], m_send.at[0], m_recv.at[j], {"expert": j}).wait_recv()
    for i in range(1, n_d):
        zi = along(i)
        remote(d_out.at[zi], d_out.at[zi], z_send.at[0], z_recv.at[zi], {"dp": zi}).wait_recv()
    for copy in sent:
        copy.wait_send()


def gather_all(trunk, gates, cot, first, second):
    n_e, n_d = lax.axis_size("expert"), lax.axis_size("dp")
    share, depth = trunk.shape
    width = first.shape[1]
    out = cot.shape[2]
    anywhere = pl.BlockSpec(memory_space=pl.ANY)
    hbm = pl.BlockSpec(memory_space=pltpu.HBM)
    vmem = pl.BlockSpec(memory_space=pltpu.VMEM)
    dma = pltpu.SemaphoreType.DMA
    return pl.pallas_call(
        functools.partial(gather_kernel, n_e, n_d),
        out_shape=(
            jax.ShapeDtypeStruct((n_d, n_e, share, depth), BF16),
            jax.ShapeDtypeStruct((n_d, n_e, share, out), BF16),
            jax.ShapeDtypeStruct((n_d, n_e * share, width), F32),
            jax.ShapeDtypeStruct(gates.shape, F32),
            jax.ShapeDtypeStruct((n_e, share, out), BF16),
        ),
        in_specs=[vmem, vmem, vmem, hbm, hbm],
        out_specs=(hbm, hbm, hbm, vmem, hbm),
        scratch_shapes=[
            pltpu.VMEM(first.shape, BF16),
            pltpu.VMEM(second.shape, BF16),
            pltpu.VMEM((n_e * share, width), BF16),
            pltpu.VMEM((n_e, share, out), BF16),
            dma((n_e,)), dma((n_e,)), dma,
            pltpu.VMEM((n_e, share, out), BF16),
            pltpu.VMEM((n_e, share, depth), BF16),
            pltpu.VMEM((n_e * share, width), F32),
            dma, dma, dma,
            dma((n_e,)), dma((n_e,)),
            dma((n_d, n_e)), dma((n_d, n_e)),
            dma((n_e,)), dma((n_e,)),
            dma((n_d,)), dma((n_d,)),
            dma((4,)),
        ],
        compiler_params=pltpu.CompilerParams(
            collective_id=0, has_side_effects=True, vmem_limit_bytes=48 * 1024 * 1024),
    )(trunk, gates, cot, first, second)


def return_kernel(n_e, d_pre, first, d_gate, d_trunk, gate_back, weights, part, near, pair, got,
                  w_sem, n_send, n_recv, p_send, p_recv, g_send, g_recv, own_sem):
    e = lax.axis_index("expert")
    core, seat, pairs = lax.rem(e, 2), e // 2, n_e // 2
    partner = e + 1 - 2 * core
    tiles, tile, _ = weights.shape

    def plane(s):
        return lax.rem(e + s, n_e)

    def remote(src, dst, send, recv, j):
        return pltpu.make_async_remote_copy(
            src_ref=src, dst_ref=dst, send_sem=send, recv_sem=recv,
            device_id={"expert": j}, device_id_type=MESH)

    def load(c):
        return pltpu.make_async_copy(first.at[c], weights.at[c], w_sem.at[c])

    for c in range(tiles):
        load(c).start()
    barrier = pltpu.get_barrier_semaphore()
    for s in range(1, n_e):
        pl.semaphore_signal(barrier, inc=1, device_id={"expert": plane(s)}, device_id_type=MESH)
    pl.semaphore_wait(barrier, n_e - 1)

    own = pltpu.make_async_copy(d_gate.at[e], gate_back.at[e], own_sem)
    own.start()

    def gate_out(s):
        j = plane(s)
        return remote(d_gate.at[j], gate_back.at[e], g_send.at[s], g_recv.at[e], j)

    def near_out(c):
        return remote(part.at[c, :, 1 - core], near.at[c], n_send.at[c], n_recv.at[c], partner)

    def part_out(c, s):
        k = lax.rem(seat + s, pairs)
        return remote(pair.at[c, k], got.at[c, seat], p_send.at[c, s], p_recv.at[c, seat],
                      2 * k + core)

    for s in range(1, n_e):
        gate_out(s).start()

    def compute(c):
        load(c).wait()
        value = lax.dot_general(
            d_pre[...], weights[c], (((1,), (1,)), ((), ())), preferred_element_type=F32)
        part[c] = value.astype(BF16).reshape(pairs, 2, -1, tile)

    def combine(c):
        near_out(c).wait_recv()
        pair[c] = (part[c, :, core].astype(F32) + near[c].astype(F32)).astype(BF16)

    def send(c):
        for s in range(1, pairs):
            part_out(c, s).start()

    compute(0)
    near_out(0).start()
    compute(1)
    combine(0)

    @pl.loop(2, tiles)
    def _(c):
        near_out(c - 1).start()
        send(c - 2)
        compute(c)
        combine(c - 1)

    near_out(tiles - 1).start()
    send(tiles - 2)
    combine(tiles - 1)
    send(tiles - 1)

    @pl.loop(0, tiles)
    def _(c):
        total = pair[c, seat].astype(F32)
        for s in range(1, pairs):
            k = lax.rem(seat + s, pairs)
            remote(pair.at[c, k], got.at[c, k], p_send.at[c, 0], p_recv.at[c, k],
                   2 * k + core).wait_recv()
            total = total + got[c, k].astype(F32)
        d_trunk[:, pl.ds(pl.multiple_of(c * tile, tile), tile)] = total.astype(BF16)

    own.wait()
    for s in range(1, n_e):
        j = plane(s)
        remote(d_gate.at[j], gate_back.at[j], g_send.at[0], g_recv.at[j], j).wait_recv()
    for s in range(1, n_e):
        gate_out(s).wait_send()

    @pl.loop(0, tiles)
    def _(c):
        near_out(c).wait_send()
        for s in range(1, pairs):
            part_out(c, s).wait_send()


def return_all(d_pre, first, d_gate):
    n_e = lax.axis_size("expert")
    tile = 512
    depth, width = first.shape
    tiles = depth // tile
    share = d_pre.shape[0] // n_e
    hbm = pl.BlockSpec(memory_space=pltpu.HBM)
    vmem = pl.BlockSpec(memory_space=pltpu.VMEM)
    dma = pltpu.SemaphoreType.DMA
    return pl.pallas_call(
        functools.partial(return_kernel, n_e),
        out_shape=(
            jax.ShapeDtypeStruct((share, depth), BF16),
            jax.ShapeDtypeStruct(d_gate.shape, F32),
        ),
        in_specs=[vmem, hbm, vmem],
        out_specs=(vmem, vmem),
        scratch_shapes=[
            pltpu.VMEM((tiles, tile, width), BF16),
            pltpu.VMEM((tiles, n_e // 2, 2, share, tile), BF16),
            pltpu.VMEM((tiles, n_e // 2, share, tile), BF16),
            pltpu.VMEM((tiles, n_e // 2, share, tile), BF16),
            pltpu.VMEM((tiles, n_e // 2, share, tile), BF16),
            dma((tiles,)), dma((tiles,)), dma((tiles,)),
            dma((tiles, n_e // 2)), dma((tiles, n_e // 2)),
            dma((n_e,)), dma((n_e,)), dma,
        ],
        compiler_params=pltpu.CompilerParams(
            collective_id=1, has_side_effects=True, vmem_limit_bytes=48 * 1024 * 1024),
    )(d_pre, first.reshape(tiles, tile, width), d_gate)


def on_device(trunk, w_first, w_second, gates, d_mixed):
    rank = lax.axis_index("dp")
    first = w_first[0]
    second = w_second[0]
    gate_here = gates[0]
    n_dp = lax.axis_size("dp")
    depth = first.shape[0] // n_dp
    units = second.shape[0] // n_dp
    group = gate_here.shape[1]

    n_e = lax.axis_size("expert")
    gate_parts = gate_here.T.astype(F32).reshape(n_e, -1, gate_here.shape[0])
    rows_all, d_output_all, pre, gates_each, outs_each = gather_all(
        trunk, gate_parts, jnp.transpose(d_mixed, (1, 0, 2)), first, second)
    rows_all = rows_all.reshape(-1, trunk.shape[1])
    d_output_all = d_output_all.reshape(-1, second.shape[1])
    pre = pre.reshape(-1, first.shape[1])
    gates_each = gates_each.astype(BF16)
    d_hidden = lax.dot_general(
        d_output_all, second, (((1,), (1,)), ((), ())), preferred_element_type=F32
    )
    sig = jax.nn.sigmoid(pre)
    d_pre = (d_hidden * sig * (1.0 + pre * (1.0 - sig))).astype(BF16)
    d_pre_here = lax.dynamic_slice_in_dim(d_pre, rank * group, group, 0)
    mixed = jnp.einsum(
        "ert,ero->rto", gates_each, outs_each, preferred_element_type=F32
    ).astype(BF16)
    d_gate_each = jnp.einsum(
        "rto,ero->ert", d_mixed, outs_each, preferred_element_type=F32
    ).astype(BF16)
    d_trunk, back_gate = return_all(d_pre_here, first, d_gate_each.astype(F32))
    d_gate = back_gate.reshape(group, -1).T.astype(BF16)[None]

    columns = lax.dynamic_slice_in_dim(rows_all, rank * depth, depth, 1)
    d_first = lax.dot_general(
        columns, d_pre, (((0,), (0,)), ((), ())), preferred_element_type=F32
    ).astype(BF16)
    some_pre = lax.dynamic_slice_in_dim(pre, rank * units, units, 1)
    some_hidden = jax.nn.silu(some_pre).astype(BF16)
    d_second = lax.dot_general(
        some_hidden, d_output_all, (((0,), (0,)), ((), ())), preferred_element_type=F32
    ).astype(BF16)
    return (mixed, d_trunk, d_gate, d_first[None], d_second[None])


def solution(mesh):
    in_specs = (
        P(("dp", "expert"), None),
        P("expert", None, None),
        P("expert", None, None),
        P("expert", None, "dp"),
        P(("dp", "expert"), None, None),
    )
    out_specs = (
        P(("dp", "expert"), None, None),
        P(("dp", "expert"), None),
        P("expert", None, "dp"),
        P("expert", "dp", None),
        P("expert", "dp", None),
    )
    return jax.shard_map(
        on_device, mesh=mesh, in_specs=in_specs, out_specs=out_specs, check_vma=False
    )
```

profile of v0, /device:TPU:8, one launch (start us, length us, event | category | flops | bytes accessed | tf_op | source)
XLA Modules:
  0.0 121.4 jit_solution(3503409141554923387)
XLA Ops:
  0.6 0.7 convert_bitcast_fusion.2
  1.3 0.1 copy.17
  1.4 1.2 %copy.32 = bf16[24,8,1024]{2,0,1:T(8,128)(2,1)S(1)} copy(bf16[24,8,1024]{2,1,0:T(8,128)(2,1)} %param.9) | data formatting | bytes 786432 | tf_op args[4]
  2.7 0.0 copy-start
  2.7 0.9 copy-done
  3.6 0.0 copy-start.2
  3.6 81.6 %shard_map.92 = (bf16[4,8,24,4096]{3,2,1,0:T(8,128)(2,1)}, bf16[4,8,24,1024]{3,2,1,0:T(8,128)(2,1)S(1)}, f32[4,192,2048]{2,1,0:T(8,128)}, f32[8,24,8]{2,1,0:T(8,128)S(1)}, bf16[8,24,1024]{2,1,0:T(8,128)(2,1)S(1)}) custom-call(bf16[24,4096]{1,0:T(8,128)(2,1)S(1)} %copy-done, f32[8,24,8]{2,1,0:T(8,128)S(1)} %bitcast.32, bf16[8,24,1024]{2,1,0:T(8,128)(2,1)S(1)} %bitcast.31, ...), custom_call_target="tpu_custom_call" | custom-call | tf_op jit(solution)/shard_map/pallas_call | solution.py:184
  85.3 0.0 copy-done.2
  85.3 0.4 fusion.3
  85.6 1.1 convolution_convert_fusion.1
  86.8 0.1 copy.22
  86.9 0.1 copy.23
  87.0 0.0 copy-start.1
  87.0 3.6 %fusion.1 = bf16[1,512,1024]{2,1,0:T(8,128)(2,1)} fusion(bf16[768,1024]{1,0:T(8,128)(2,1)S(1)} %bitcast.33, f32[768,2048]{1,0:T(8,128)} %bitcast.41, s32[]{:T(128)S(6)} %select_n.11), kind=kOutput, calls=%fused_computation.5 | convolution fusion | flops 807796736 | bytes 4194308 | tf_op jit(solution)/shard_map/dot_general | solution.py:385
  90.6 0.0 copy-done.1
  90.6 6.7 %multiply_convert_fusion = bf16[768,2048]{1,0:T(8,128)(2,1)S(1)} fusion(f32[768,2048]{1,0:T(8,128)} %bitcast.42, bf16[768,1024]{1,0:T(8,128)(2,1)S(1)} %bitcast.34, bf16[1,2048,1024]{2,1,0:T(8,128)(2,1)S(1)} %copy-done.1), kind=kOutput, calls=%fused_computation | convolution fusion | flops 3235381248 | bytes 15204352 | tf_op jit(solution)/shard_map/dot_general | solution.py:364
  97.3 6.4 %convert_bitcast_fusion = bf16[1,1024,2048]{2,1,0:T(8,128)(2,1)} fusion(bf16[768,2048]{1,0:T(8,128)(2,1)S(1)} %multiply_convert_fusion, bf16[768,4096]{1,0:T(8,128)(2,1)} %bitcast.40, s32[]{:T(128)S(6)} %select_n.10), kind=kOutput, calls=%fused_computation.1 | convolution fusion | flops 3223322624 | bytes 8912900 | tf_op jit(solution)/shard_map/dot_general | solution.py:380
  103.8 0.1 constant_dynamic-slice_fusion.d_pre
  103.8 16.2 %shard_map.93 = (bf16[24,4096]{1,0:T(8,128)(2,1)S(1)}, f32[8,24,8]{2,1,0:T(8,128)S(1)}) custom-call(bf16[192,2048]{1,0:T(8,128)(2,1)S(1)} %constant_dynamic-slice_fusion.d_pre, bf16[8,512,2048]{2,1,0:T(8,128)(2,1)} %bitcast.36, f32[8,24,8]{2,1,0:T(8,128)S(1)} %convert_bitcast_fusion.1.d_gate), custom_call_target="tpu_custom_call" | custom-call | tf_op jit(solution)/shard_map/pallas_call | solution.py:323
  120.1 0.7 copy.24
  120.7 0.7 copy.34
  (3 shorter events, 0.0 us)
Async XLA Ops:
  2.7 0.9 copy-start
  3.6 81.7 %copy-start.2 = (bf16[24,8,1024]{2,1,0:T(8,128)(2,1)S(1)}, bf16[24,8,1024]{2,1,0:T(8,128)(2,1)}, u32[]{:S(2)}) copy-start(bf16[24,8,1024]{2,1,0:T(8,128)(2,1)} %param.9) | copy-start | bytes 1179652
  87.0 3.6 %copy-start.1 = (bf16[1,2048,1024]{2,1,0:T(8,128)(2,1)S(1)}, bf16[1,2048,1024]{2,1,0:T(8,128)(2,1)}, u32[]{:S(2)}) copy-start(bf16[1,2048,1024]{2,1,0:T(8,128)(2,1)} %param.7) | copy-start | bytes 12582916
where the time goes:
time: 122 us; the launch traced here: 121 us
  Pallas kernels  97.8 us (80%)
  matrix products  18.3 us (15%)
  local copies, waits for them, and re-layouts  3.86 us (3%)
    pallas_call x1, Pallas kernels, gather_all(): pl.pallas_call(functools.partial(gather_kernel, n_e, n_d), out_shape=(jax...  81.6 us
    pallas_call x1, Pallas kernels, return_all(): pl.pallas_call(functools.partial(return_kernel, n_e), out_shape=(jax.Shap...  16.2 us
    dot_general x1, matrix products, on_device(): lax.dot_general(d_output_all, second, (((1,), (1,)), ((), ())), preferred...  6.74 us
    dot_general x1, matrix products, on_device(): lax.dot_general(columns, d_pre, (((0,), (0,)), ((), ())), preferred_eleme...  6.44 us
    dot_general x1, matrix products, on_device(): lax.dot_general(some_hidden, d_output_all, (((0,), (0,)), ((), ())), pref...  3.58 us
    unnamed x8, local copies, waits for them, and re-layouts  2.83 us

commit v1 on v0

--- a/solution.py
+++ b/solution.py
@@ -388,6 +388,478 @@
     return (mixed, d_trunk, d_gate, d_first[None], d_second[None])
 
 
+SIDE, LINE, LANES = 2, 4, 128
+
+
+def tiled(count, body, hooks=()):
+    @pl.loop(0, count)
+    def _(c):
+        body(c)
+        for at, hook in hooks:
+            pl.when(c == at)(hook)
+
+
+def step_kernel(n_e, n_d, trunk, gates, cot_in, first, second,
+                rows, d_out, d_pre, some_hidden, mixed, d_trunk, gate_back,
+                weights, later, cot, gate_each, mix, piece, tall, hidden, made, outs, d_gate,
+                part, near, pair, got,
+                load_sem, own_sem, g_send, g_recv, t_send, t_recv, o_send, o_recv, z_send, z_recv,
+                m_send, m_recv, n_send, n_recv, p_send, p_recv, b_send, b_recv):
+    e = lax.axis_index("expert")
+    z = lax.axis_index("dp")
+    core, seat, pairs = lax.rem(e, 2), e // 2, n_e // 2
+    partner = e + 1 - 2 * core
+    side, up = lax.rem(seat, SIDE), seat // SIDE
+    across = e + 2 - 4 * side
+    over = e + 2 * SIDE - 4 * SIDE * up
+    corner = across + over - e
+    bridge = across * (1 - core) + over * core
+    other = across * core + over * (1 - core)
+    middle = (z * (n_d - 1 - z)) // 2
+    inner = middle == 1
+    mate = z + 1 - 2 * lax.rem(z, 2)
+    mirror = n_d - 1 - z
+    skip = lax.rem(z + 2, n_d)
+    order = [z, mate, middle * mirror + (1 - middle) * skip, middle * skip + (1 - middle) * mirror]
+    tasks = cot.shape[0] // rows.shape[2]
+    share, depth = rows.shape[2], rows.shape[3]
+    width = tall.shape[2]
+    group = n_e * share
+    units = some_hidden.shape[2]
+
+    def plane(s):
+        return lax.rem(e + s, n_e)
+
+    def remote(src, dst, send, recv, where):
+        return pltpu.make_async_remote_copy(
+            src_ref=src, dst_ref=dst, send_sem=send, recv_sem=recv,
+            device_id=where, device_id_type=MESH)
+
+    def load(k):
+        src, dst = [(second, later), (cot_in, cot), (first, weights)][k]
+        return pltpu.make_async_copy(src, dst, load_sem.at[k])
+
+    def own(k):
+        src, dst = [(gates.at[e], gate_each.at[e]), (trunk, rows.at[z, e]),
+                    (piece.at[e], d_out.at[z, e]), (made.at[e], outs.at[e]),
+                    (d_gate.at[e], gate_back.at[e])][k]
+        return pltpu.make_async_copy(src, dst, own_sem.at[k])
+
+    def at_plane(j):
+        return {"expert": j}
+
+    def gate_out(s):
+        j = plane(s)
+        return remote(gates.at[j], gate_each.at[e], g_send.at[s], g_recv.at[e], at_plane(j))
+
+    def trunk_out(g, k):
+        zi = order[g]
+        j, where = [
+            (e, at_plane(across)), (e, at_plane(over)), (e, at_plane(partner)),
+            (bridge, at_plane(over * (1 - core) + across * core)),
+            (bridge, at_plane(partner)), (other, at_plane(partner)), (corner, at_plane(partner)),
+            (e, {"dp": mate}), (e, {"dp": mirror})][k]
+        src = trunk if g == 0 and k in (0, 1, 2, 7, 8) else rows.at[zi, j]
+        return remote(src, rows.at[zi, j], t_send.at[g, k], t_recv.at[zi, j], where)
+
+    def trunk_in(g, j):
+        zi = order[g]
+        remote(trunk, rows.at[zi, j], t_send.at[0, 0], t_recv.at[zi, j],
+               at_plane(partner)).wait_recv()
+
+    def piece_out(s):
+        j = plane(s)
+        return remote(piece.at[j], d_out.at[z, e], o_send.at[s], o_recv.at[e], at_plane(j))
+
+    def line_out(g, k):
+        zi = order[g]
+        return remote(d_out.at[zi], d_out.at[zi], z_send.at[g, k], z_recv.at[zi],
+                      {"dp": mate if k == 0 else mirror})
+
+    def made_out(s):
+        j = plane(s)
+        return remote(made.at[j], outs.at[e], m_send.at[s], m_recv.at[e], at_plane(j))
+
+    def back_out(s):
+        j = plane(s)
+        return remote(d_gate.at[j], gate_back.at[e], b_send.at[s], b_recv.at[e], at_plane(j))
+
+    def near_out(c):
+        return remote(part.at[c, :, 1 - core], near.at[c], n_send.at[c], n_recv.at[c],
+                      at_plane(partner))
+
+    def part_out(c, s):
+        k = lax.rem(seat + s, pairs)
+        return remote(pair.at[c, k], got.at[c, seat], p_send.at[c, s], p_recv.at[c, seat],
+                      at_plane(2 * k + core))
+
+    def spread(g):
+        for k in range(3):
+            trunk_out(g, k).start()
+
+    def bridge_on(g):
+        trunk_in(g, bridge)
+        trunk_out(g, 3).start()
+        trunk_out(g, 4).start()
+        trunk_in(g, other)
+        trunk_out(g, 5).start()
+
+    def corner_on(g):
+        trunk_in(g, corner)
+        trunk_out(g, 6).start()
+
+    def complete(g):
+        for shift in (0, across - e, over - e, corner - e):
+            trunk_in(g, partner + shift)
+
+    def arrive(g):
+        trunk_in(g, e)
+        if g == 1:
+            pl.when(inner)(lambda: trunk_out(1, 8).start())
+        else:
+            pl.when(inner)(lambda: trunk_out(g, 7).start())
+
+    def line_in(g):
+        zi = order[g]
+        remote(d_out.at[zi], d_out.at[zi], z_send.at[0, 0], z_recv.at[zi],
+               {"dp": mate}).wait_recv()
+
+    def line_arrive(g):
+        line_in(g)
+        pl.when(inner)(lambda: line_out(g, 1 if g == 1 else 0).start())
+
+    def in_middle(call, g):
+        pl.when(inner)(lambda: call(g))
+
+    def at_end(call, g):
+        pl.when(middle == 0)(lambda: call(g))
+
+    for k in range(3):
+        load(k).start()
+    barrier = pltpu.get_barrier_semaphore()
+    for s in range(1, n_e):
+        pl.semaphore_signal(barrier, inc=1, device_id=at_plane(plane(s)), device_id_type=MESH)
+    for i in range(1, n_d):
+        pl.semaphore_signal(barrier, inc=1, device_id={"dp": lax.rem(z + i, n_d)},
+                            device_id_type=MESH)
+    pl.semaphore_wait(barrier, n_e - 1 + n_d - 1)
+
+    for s in range(1, n_e):
+        gate_out(s).start()
+    own(0).start()
+    own(1).start()
+    trunk_out(0, 7).start()
+    pl.when(inner)(lambda: trunk_out(0, 8).start())
+    spread(0)
+
+    def task_of():
+        shape = (LANES, share * tasks)
+        return jnp.where(
+            lax.broadcasted_iota(jnp.int32, shape, 0)
+            == lax.rem(lax.broadcasted_iota(jnp.int32, shape, 1), tasks), 1.0, 0.0).astype(BF16)
+
+    def same_sample():
+        shape = (n_e, share, share * tasks)
+        match = (lax.broadcasted_iota(jnp.int32, shape, 1)
+                 == lax.div(lax.broadcasted_iota(jnp.int32, shape, 2), tasks))
+        return jnp.where(match, 1.0, 0.0).reshape(group, share * tasks)
+
+    for s in range(1, n_e):
+        j = plane(s)
+        remote(gates.at[j], gate_each.at[j], g_send.at[0], g_recv.at[j],
+               at_plane(j)).wait_recv()
+    own(0).wait()
+    load(1).wait()
+    each = gate_each[...].reshape(group, LANES).astype(BF16)
+    mix[...] = (jnp.dot(each, task_of(), preferred_element_type=F32)
+                * same_sample()).astype(BF16)
+    piece[...] = jnp.dot(mix[...], cot[...], preferred_element_type=F32).astype(BF16).reshape(
+        piece.shape)
+    for s in range(1, n_e):
+        piece_out(s).start()
+    own(2).start()
+
+    bridge_on(0)
+    arrive(1)
+    in_middle(arrive, 2)
+    for s in range(1, n_e):
+        j = plane(s)
+        remote(piece.at[j], d_out.at[z, j], o_send.at[0], o_recv.at[j], at_plane(j)).wait_recv()
+    own(2).wait()
+    line_out(0, 0).start()
+    pl.when(inner)(lambda: line_out(0, 1).start())
+    spread(1)
+
+    tile = 512
+
+    def part_of(c):
+        return pl.ds(pl.multiple_of(c * tile, tile), tile)
+
+    def back_hidden(g, c):
+        left = d_out[order[g]].reshape(group, d_out.shape[3])
+        return lax.dot_general(left, later[part_of(c), :], (((1,), (1,)), ((), ())),
+                               preferred_element_type=F32)
+
+    def forward_pre(g, c):
+        left = rows[order[g]].reshape(group, depth)
+        return jnp.dot(left, weights[:, part_of(c)], preferred_element_type=F32)
+
+    def store_d_pre(g, c, d_hidden, value):
+        sig = jax.nn.sigmoid(value)
+        d_pre[order[g], :, part_of(c)] = (
+            d_hidden * sig * (1.0 + value * (1.0 - sig))).astype(BF16)
+        return sig
+
+    def first_hidden(c):
+        tall[0, :, part_of(c)] = back_hidden(0, c)
+
+    def first_pre(c):
+        value = forward_pre(0, c)
+        sig = store_d_pre(0, c, tall[0, :, part_of(c)], value)
+        hidden[:, part_of(c)] = (value * sig).astype(BF16)
+
+    def later_pre(g):
+        def body(c):
+            tall[g, :, part_of(c)] = forward_pre(g, c)
+        return body
+
+    def later_hidden(g):
+        def body(c):
+            store_d_pre(g, c, back_hidden(g, c), tall[g, :, part_of(c)])
+        return body
+
+    units_here = pl.ds(pl.multiple_of(z * units, units), units)
+
+    def keep_units(g):
+        value = tall[g, :, units_here]
+        some_hidden[order[g]] = (value * jax.nn.sigmoid(value)).astype(BF16)
+
+    load(0).wait()
+    tiled(width // tile, first_hidden)
+    corner_on(0)
+    own(1).wait()
+    complete(0)
+    load(2).wait()
+
+    def hook_a():
+        in_middle(arrive, 3)
+        at_end(arrive, 2)
+        spread(2)
+
+    tiled(width // tile, first_pre, [(1, hook_a)])
+    some_hidden[z] = hidden[:, units_here]
+    bridge_on(1)
+
+    def first_output(c):
+        value = jnp.dot(hidden[...], later[:, part_of(c)], preferred_element_type=F32)
+        made[:, :, part_of(c)] = value.astype(BF16).reshape(n_e, share, tile)
+
+    tiled(made.shape[2] // tile, first_output)
+    own(3).start()
+    for s in range(1, n_e):
+        made_out(s).start()
+
+    def compute(c):
+        value = lax.dot_general(d_pre[z], weights[part_of(c), :], (((1,), (1,)), ((), ())),
+                                preferred_element_type=F32)
+        part[c] = value.astype(BF16).reshape(pairs, 2, share, tile)
+
+    def combine(c):
+        near_out(c).wait_recv()
+        pair[c] = (part[c, :, core].astype(F32) + near[c].astype(F32)).astype(BF16)
+
+    def send(c):
+        for s in range(1, pairs):
+            part_out(c, s).start()
+
+    count = depth // tile
+    compute(0)
+    near_out(0).start()
+    compute(1)
+    combine(0)
+    corner_on(1)
+
+    def hook_b():
+        line_arrive(1)
+        in_middle(line_arrive, 2)
+
+    def hook_c():
+        at_end(arrive, 3)
+        spread(3)
+
+    def middle_tile(c):
+        near_out(c - 1).start()
+        send(c - 2)
+        compute(c)
+        combine(c - 1)
+
+    hooks = [(2, hook_b), (3, lambda: bridge_on(2)), (4, hook_c)]
+
+    @pl.loop(2, count)
+    def _(c):
+        middle_tile(c)
+        for at, hook in hooks:
+            pl.when(c == at)(hook)
+
+    near_out(count - 1).start()
+    send(count - 2)
+    combine(count - 1)
+    send(count - 1)
+    complete(1)
+    tiled(width // tile, later_pre(1), [(1, lambda: corner_on(2))])
+
+    def hook_d():
+        in_middle(line_arrive, 3)
+        at_end(line_arrive, 2)
+
+    tiled(width // tile, later_hidden(1), [(1, lambda: bridge_on(3))])
+    keep_units(1)
+    complete(2)
+    tiled(width // tile, later_pre(2), [(1, hook_d), (2, lambda: corner_on(3))])
+    keep_units(2)
+    tiled(width // tile, later_hidden(2))
+    complete(3)
+    tiled(width // tile, later_pre(3))
+    keep_units(3)
+
+    own(3).wait()
+    for s in range(1, n_e):
+        j = plane(s)
+        remote(made.at[j], outs.at[j], m_send.at[0], m_recv.at[j], at_plane(j)).wait_recv()
+    each_out = outs[...].reshape(group, outs.shape[2])
+    product = lax.dot_general(each_out, cot[...], (((1,), (1,)), ((), ())),
+                              preferred_element_type=F32)
+    product = (product * same_sample()).astype(BF16)
+    d_gate[...] = lax.dot_general(product, task_of(), (((1,), (1,)), ((), ())),
+                                  preferred_element_type=F32).reshape(d_gate.shape)
+    own(4).start()
+    for s in range(1, n_e):
+        back_out(s).start()
+    mixed[...] = lax.dot_general(mix[...], each_out, (((0,), (0,)), ((), ())),
+                                 preferred_element_type=F32).astype(BF16)
+
+    @pl.loop(0, count)
+    def _(c):
+        total = pair[c, seat].astype(F32)
+        for s in range(1, pairs):
+            k = lax.rem(seat + s, pairs)
+            remote(pair.at[c, k], got.at[c, k], p_send.at[c, 0], p_recv.at[c, k],
+                   at_plane(2 * k + core)).wait_recv()
+            total = total + got[c, k].astype(F32)
+        d_trunk[:, part_of(c)] = total.astype(BF16)
+
+    at_end(line_arrive, 3)
+    tiled(width // tile, later_hidden(3))
+
+    own(4).wait()
+    for s in range(1, n_e):
+        j = plane(s)
+        remote(d_gate.at[j], gate_back.at[j], b_send.at[0], b_recv.at[j], at_plane(j)).wait_recv()
+    for s in range(1, n_e):
+        gate_out(s).wait_send()
+        piece_out(s).wait_send()
+        made_out(s).wait_send()
+        back_out(s).wait_send()
+    for g in range(n_d):
+        for k in range(7):
+            trunk_out(g, k).wait_send()
+    trunk_out(0, 7).wait_send()
+    line_out(0, 0).wait_send()
+
+    @pl.when(inner)
+    def _():
+        trunk_out(0, 8).wait_send()
+        line_out(0, 1).wait_send()
+        trunk_out(1, 8).wait_send()
+        line_out(1, 1).wait_send()
+        for g in range(2, n_d):
+            trunk_out(g, 7).wait_send()
+            line_out(g, 0).wait_send()
+
+    @pl.loop(0, count)
+    def _(c):
+        near_out(c).wait_send()
+        for s in range(1, pairs):
+            part_out(c, s).wait_send()
+
+
+def step_all(trunk, gates, cot, first, second):
+    n_e, n_d = lax.axis_size("expert"), lax.axis_size("dp")
+    share, depth = trunk.shape
+    width = first.shape[1]
+    out = second.shape[1]
+    group = n_e * share
+    count, pairs, tile = depth // 512, n_e // 2, 512
+    anywhere = pl.BlockSpec(memory_space=pl.ANY)
+    hbm = pl.BlockSpec(memory_space=pltpu.HBM)
+    vmem = pl.BlockSpec(memory_space=pltpu.VMEM)
+    dma = pltpu.SemaphoreType.DMA
+    return pl.pallas_call(
+        functools.partial(step_kernel, n_e, n_d),
+        out_shape=(
+            jax.ShapeDtypeStruct((n_d, n_e, share, depth), BF16),
+            jax.ShapeDtypeStruct((n_d, n_e, share, out), BF16),
+            jax.ShapeDtypeStruct((n_d, group, width), BF16),
+            jax.ShapeDtypeStruct((n_d, group, width // n_d), BF16),
+            jax.ShapeDtypeStruct((cot.shape[0], out), BF16),
+            jax.ShapeDtypeStruct((share, depth), BF16),
+            jax.ShapeDtypeStruct(gates.shape, F32),
+        ),
+        in_specs=[hbm, vmem, hbm, hbm, hbm],
+        out_specs=(vmem,) * 7,
+        scratch_shapes=[
+            pltpu.VMEM(first.shape, BF16),
+            pltpu.VMEM(second.shape, BF16),
+            pltpu.VMEM(cot.shape, BF16),
+            pltpu.VMEM(gates.shape, F32),
+            pltpu.VMEM((group, cot.shape[0]), BF16),
+            pltpu.VMEM((n_e, share, out), BF16),
+            pltpu.VMEM((n_d, group, width), F32),
+            pltpu.VMEM((group, width), BF16),
+            pltpu.VMEM((n_e, share, out), BF16),
+            pltpu.VMEM((n_e, share, out), BF16),
+            pltpu.VMEM(gates.shape, F32),
+            pltpu.VMEM((count, pairs, 2, share, tile), BF16),
+            pltpu.VMEM((count, pairs, share, tile), BF16),
+            pltpu.VMEM((count, pairs, share, tile), BF16),
+            pltpu.VMEM((count, pairs, share, tile), BF16),
+            dma((3,)), dma((5,)),
+            dma((n_e,)), dma((n_e,)),
+            dma((n_d, 9)), dma((n_d, n_e)),
+            dma((n_e,)), dma((n_e,)),
+            dma((n_d, 2)), dma((n_d,)),
+            dma((n_e,)), dma((n_e,)),
+            dma((count,)), dma((count,)),
+            dma((count, pairs)), dma((count, pairs)),
+            dma((n_e,)), dma((n_e,)),
+        ],
+        compiler_params=pltpu.CompilerParams(
+            collective_id=2, has_side_effects=True, vmem_limit_bytes=48 * 1024 * 1024),
+    )(trunk, gates, cot, first, second)
+
+
+def on_square(trunk, w_first, w_second, gates, d_mixed):
+    rank = lax.axis_index("dp")
+    n_e, n_d = lax.axis_size("expert"), lax.axis_size("dp")
+    first, second, gate_here = w_first[0], w_second[0], gates[0]
+    tasks, group = gate_here.shape
+    share = group // n_e
+    depth = first.shape[0] // n_d
+    gate_parts = jnp.pad(gate_here.T.astype(F32).reshape(n_e, share, tasks),
+                         ((0, 0), (0, 0), (0, LANES - tasks)))
+    rows, d_out, d_pre, some_hidden, mixed, d_trunk, back = step_all(
+        trunk, gate_parts, d_mixed.reshape(share * tasks, -1), first, second)
+    d_gate = back[:, :, :tasks].reshape(group, tasks).T.astype(BF16)[None]
+    columns = lax.dynamic_slice_in_dim(rows.reshape(-1, first.shape[0]), rank * depth, depth, 1)
+    d_first = lax.dot_general(
+        columns, d_pre.reshape(-1, first.shape[1]), (((0,), (0,)), ((), ())),
+        preferred_element_type=F32).astype(BF16)
+    d_second = lax.dot_general(
+        some_hidden.reshape(-1, some_hidden.shape[2]), d_out.reshape(-1, second.shape[1]),
+        (((0,), (0,)), ((), ())), preferred_element_type=F32).astype(BF16)
+    return (mixed.reshape(d_mixed.shape), d_trunk, d_gate, d_first[None], d_second[None])
+
+
 def solution(mesh):
     in_specs = (
         P(("dp", "expert"), None),
@@ -403,6 +875,7 @@
         P("expert", "dp", None),
         P("expert", "dp", None),
     )
+    fits = mesh.shape["expert"] == 2 * SIDE * SIDE and mesh.shape["dp"] == LINE
     return jax.shard_map(
-        on_device, mesh=mesh, in_specs=in_specs, out_specs=out_specs, check_vma=False
+        on_square if fits else on_device, mesh=mesh, in_specs=in_specs, out_specs=out_specs, check_vma=False
     )

time: 122 us -> 83.9 us (0.69)
  the two profiles are of different devices: /device:TPU:8 before, /device:TPU:0 now
where the time goes in v1:
time: 83.9 us; the launch traced here: 83.7 us
  Pallas kernels  69.7 us (83%)
  matrix products  8.45 us (10%)
  local copies, waits for them, and re-layouts  4.84 us (6%)
    pallas_call x1, Pallas kernels, step_all(): pl.pallas_call(functools.partial(step_kernel, n_e, n_d), out_shape=(jax.S...  69.7 us
    dot_general x1, matrix products, on_square(): lax.dot_general(columns, d_pre.reshape(-1, first.shape[1]), (((0,), (0,))...  6.48 us
    unnamed x8, local copies, waits for them, and re-layouts  3.34 us
    dot_general x1, matrix products, on_square(): lax.dot_general(some_hidden.reshape(-1, some_hidden.shape[2]), d_out.resh...  1.97 us

profile of v1, /device:TPU:0, one launch (start us, length us, event | category | flops | bytes accessed | tf_op | source)
XLA Modules:
  0.0 83.7 jit_solution(16019835357777840836)
XLA Ops:
  0.6 0.8 copy.10
  1.5 0.0 copy-start
  1.5 1.0 %copy-done = bf16[24,8,1024]{2,1,0:T(8,128)(2,1)S(1)} copy-done((bf16[24,8,1024]{2,1,0:T(8,128)(2,1)S(1)}, bf16[24,8,1024]{2,1,0:T(8,128)(2,1)}, u32[]{:S(2)}) %copy-start) | copy-done | bytes 393240
  2.5 0.0 copy-start.1
  2.5 0.9 %copy-done.1 = bf16[24,4096]{1,0:T(8,128)(2,1)S(1)} copy-done((bf16[24,4096]{1,0:T(8,128)(2,1)S(1)}, bf16[24,4096]{1,0:T(8,128)(2,1)}, u32[]{:S(2)}) %copy-start.1) | copy-done | bytes 196632
  3.4 69.7 %shard_map.92 = (bf16[4,8,24,4096]{3,2,1,0:T(8,128)(2,1)}, bf16[4,8,24,1024]{3,2,1,0:T(8,128)(2,1)S(1)}, bf16[4,192,2048]{2,1,0:T(8,128)(2,1)}, bf16[4,192,512]{...) custom-call(bf16[24,4096]{1,0:T(8,128)(2,1)S(1)} %copy-done.1, ...), custom_call_target="tpu_custom_call" | custom-call | tf_op jit(solution)/shard_map/pallas_call | solution.py:797
  73.1 0.7 copy.11
  73.8 0.0 copy-start.2
  73.8 2.0 %fusion.1 = bf16[1,512,1024]{2,1,0:T(8,128)(2,1)} fusion(bf16[768,512]{1,0:T(8,128)(2,1)S(1)} %bitcast.26, bf16[768,1024]{1,0:T(8,128)(2,1)S(1)} %bitcast.25), kind=kOutput, calls=%fused_computation.3 | convolution fusion | flops 805830656 | bytes 3407872 | tf_op jit(solution)/shard_map/dot_general | solution.py:857
  75.8 0.0 copy-done.2
  75.8 6.5 %convert_bitcast_fusion = bf16[1,1024,2048]{2,1,0:T(8,128)(2,1)} fusion(bf16[768,2048]{1,0:T(8,128)(2,1)S(1)} %bitcast.34, bf16[768,4096]{1,0:T(8,128)(2,1)} %bitcast.33, s32[]{:T(128)S(6)} %select_n.3), kind=kOutput, calls=%fused_computation | convolution fusion | flops 3223322624 | bytes 8912900 | tf_op jit(solution)/shard_map/dot_general | solution.py:854
  82.3 0.7 copy.14
  83.0 0.7 copy.15
  (2 shorter events, 0.0 us)
Async XLA Ops:
  1.5 1.0 %copy-start = (bf16[24,8,1024]{2,1,0:T(8,128)(2,1)S(1)}, bf16[24,8,1024]{2,1,0:T(8,128)(2,1)}, u32[]{:S(2)}) copy-start(bf16[24,8,1024]{2,1,0:T(8,128)(2,1)} %param.9) | copy-start | bytes 1179652
  2.5 0.9 %copy-start.1 = (bf16[24,4096]{1,0:T(8,128)(2,1)S(1)}, bf16[24,4096]{1,0:T(8,128)(2,1)}, u32[]{:S(2)}) copy-start(bf16[24,4096]{1,0:T(8,128)(2,1)} %trunk.1) | copy-start | bytes 589828
  73.8 2.0 %copy-start.2 = (bf16[4,192,2048]{2,1,0:T(8,128)(2,1)S(1)}, bf16[4,192,2048]{2,1,0:T(8,128)(2,1)}, u32[]{:S(2)}) copy-start(bf16[4,192,2048]{2,1,0:T(8,128)(2,1)} %get-tuple-element.16) | copy-start | bytes 9437188

commit v2 on v1

--- a/solution.py
+++ b/solution.py
@@ -389,6 +389,7 @@
 
 
 SIDE, LINE, LANES = 2, 4, 128
+VMEM_BYTES = 62 * 1024 * 1024
 
 
 def tiled(count, body, hooks=()):
@@ -400,11 +401,12 @@
 
 
 def step_kernel(n_e, n_d, trunk, gates, cot_in, first, second,
-                rows, d_out, d_pre, some_hidden, mixed, d_trunk, gate_back,
+                columns_out, d_out_out, d_pre_out, units_out, mixed_out, d_trunk_out, back_out_ref,
+                rows, d_out, d_pre, some_hidden, mixed, d_trunk, gate_back, gate_in, gate_piece,
                 weights, later, cot, gate_each, mix, piece, tall, hidden, made, outs, d_gate,
                 part, near, pair, got,
                 load_sem, own_sem, g_send, g_recv, t_send, t_recv, o_send, o_recv, z_send, z_recv,
-                m_send, m_recv, n_send, n_recv, p_send, p_recv, b_send, b_recv):
+                m_send, m_recv, n_send, n_recv, p_send, p_recv, b_send, b_recv, out_sem):
     e = lax.axis_index("expert")
     z = lax.axis_index("dp")
     core, seat, pairs = lax.rem(e, 2), e // 2, n_e // 2
@@ -426,6 +428,8 @@
     width = tall.shape[2]
     group = n_e * share
     units = some_hidden.shape[2]
+    part_depth = depth // n_d
+    depth_here = pl.ds(pl.multiple_of(z * part_depth, part_depth), part_depth)
 
     def plane(s):
         return lax.rem(e + s, n_e)
@@ -436,11 +440,11 @@
             device_id=where, device_id_type=MESH)
 
     def load(k):
-        src, dst = [(second, later), (cot_in, cot), (first, weights)][k]
+        src, dst = [(second, later), (cot_in, cot), (first, weights), (gates, gate_in)][k]
         return pltpu.make_async_copy(src, dst, load_sem.at[k])
 
     def own(k):
-        src, dst = [(gates.at[e], gate_each.at[e]), (trunk, rows.at[z, e]),
+        src, dst = [(gate_piece.at[e], gate_each.at[e]), (trunk, rows.at[z, e]),
                     (piece.at[e], d_out.at[z, e]), (made.at[e], outs.at[e]),
                     (d_gate.at[e], gate_back.at[e])][k]
         return pltpu.make_async_copy(src, dst, own_sem.at[k])
@@ -450,7 +454,7 @@
 
     def gate_out(s):
         j = plane(s)
-        return remote(gates.at[j], gate_each.at[e], g_send.at[s], g_recv.at[e], at_plane(j))
+        return remote(gate_piece.at[j], gate_each.at[e], g_send.at[s], g_recv.at[e], at_plane(j))
 
     def trunk_out(g, k):
         zi = order[g]
@@ -471,10 +475,20 @@
         j = plane(s)
         return remote(piece.at[j], d_out.at[z, e], o_send.at[s], o_recv.at[e], at_plane(j))
 
-    def line_out(g, k):
+    def half(zi, h):
+        return d_out.at[zi, h * (n_e // 2):(h + 1) * (n_e // 2)]
+
+    def line_out(g, k, h):
         zi = order[g]
-        return remote(d_out.at[zi], d_out.at[zi], z_send.at[g, k], z_recv.at[zi],
+        return remote(half(zi, h), half(zi, h), z_send.at[g, k, h], z_recv.at[zi, h],
                       {"dp": mate if k == 0 else mirror})
+
+    def keep(k):
+        src, dst = ([(rows.at[zi, :, :, depth_here], columns_out.at[zi]) for zi in order]
+                    + [(d_pre.at[zi], d_pre_out.at[zi]) for zi in order]
+                    + [(d_out, d_out_out), (some_hidden, units_out), (mixed, mixed_out),
+                       (d_trunk, d_trunk_out), (gate_back, back_out_ref)])[k]
+        return pltpu.make_async_copy(src, dst, out_sem.at[k])
 
     def made_out(s):
         j = plane(s)
@@ -519,22 +533,19 @@
         else:
             pl.when(inner)(lambda: trunk_out(g, 7).start())
 
-    def line_in(g):
+    def line_arrive(g, h):
         zi = order[g]
-        remote(d_out.at[zi], d_out.at[zi], z_send.at[0, 0], z_recv.at[zi],
+        remote(half(zi, h), half(zi, h), z_send.at[0, 0, h], z_recv.at[zi, h],
                {"dp": mate}).wait_recv()
-
-    def line_arrive(g):
-        line_in(g)
-        pl.when(inner)(lambda: line_out(g, 1 if g == 1 else 0).start())
-
-    def in_middle(call, g):
-        pl.when(inner)(lambda: call(g))
-
-    def at_end(call, g):
-        pl.when(middle == 0)(lambda: call(g))
-
-    for k in range(3):
+        pl.when(inner)(lambda: line_out(g, 1 if g == 1 else 0, h).start())
+
+    def in_middle(call, *g):
+        pl.when(inner)(lambda: call(*g))
+
+    def at_end(call, *g):
+        pl.when(middle == 0)(lambda: call(*g))
+
+    for k in (3, 1, 0, 2):
         load(k).start()
     barrier = pltpu.get_barrier_semaphore()
     for s in range(1, n_e):
@@ -542,12 +553,19 @@
     for i in range(1, n_d):
         pl.semaphore_signal(barrier, inc=1, device_id={"dp": lax.rem(z + i, n_d)},
                             device_id_type=MESH)
-    pl.semaphore_wait(barrier, n_e - 1 + n_d - 1)
-
-    for s in range(1, n_e):
-        gate_out(s).start()
+    load(3).wait()
+    task_eye = jnp.where(
+        lax.broadcasted_iota(jnp.int32, (tasks, LANES), 0)
+        == lax.broadcasted_iota(jnp.int32, (tasks, LANES), 1), 1.0, 0.0).astype(BF16)
+    gate_piece[...] = lax.dot_general(
+        gate_in[...], task_eye, (((0,), (0,)), ((), ())),
+        preferred_element_type=F32).reshape(gate_piece.shape)
     own(0).start()
     own(1).start()
+    pl.semaphore_wait(barrier, n_e - 1 + n_d - 1)
+
+    for s in range(1, n_e):
+        gate_out(s).start()
     trunk_out(0, 7).start()
     pl.when(inner)(lambda: trunk_out(0, 8).start())
     spread(0)
@@ -566,7 +584,7 @@
 
     for s in range(1, n_e):
         j = plane(s)
-        remote(gates.at[j], gate_each.at[j], g_send.at[0], g_recv.at[j],
+        remote(gate_piece.at[j], gate_each.at[j], g_send.at[0], g_recv.at[j],
                at_plane(j)).wait_recv()
     own(0).wait()
     load(1).wait()
@@ -575,20 +593,12 @@
                 * same_sample()).astype(BF16)
     piece[...] = jnp.dot(mix[...], cot[...], preferred_element_type=F32).astype(BF16).reshape(
         piece.shape)
+    bridge_on(0)
     for s in range(1, n_e):
         piece_out(s).start()
     own(2).start()
-
-    bridge_on(0)
     arrive(1)
     in_middle(arrive, 2)
-    for s in range(1, n_e):
-        j = plane(s)
-        remote(piece.at[j], d_out.at[z, j], o_send.at[0], o_recv.at[j], at_plane(j)).wait_recv()
-    own(2).wait()
-    line_out(0, 0).start()
-    pl.when(inner)(lambda: line_out(0, 1).start())
-    spread(1)
 
     tile = 512
 
@@ -608,15 +618,11 @@
         sig = jax.nn.sigmoid(value)
         d_pre[order[g], :, part_of(c)] = (
             d_hidden * sig * (1.0 + value * (1.0 - sig))).astype(BF16)
-        return sig
-
-    def first_hidden(c):
-        tall[0, :, part_of(c)] = back_hidden(0, c)
 
     def first_pre(c):
         value = forward_pre(0, c)
-        sig = store_d_pre(0, c, tall[0, :, part_of(c)], value)
-        hidden[:, part_of(c)] = (value * sig).astype(BF16)
+        tall[0, :, part_of(c)] = value
+        hidden[:, part_of(c)] = (value * jax.nn.sigmoid(value)).astype(BF16)
 
     def later_pre(g):
         def body(c):
@@ -634,21 +640,29 @@
         value = tall[g, :, units_here]
         some_hidden[order[g]] = (value * jax.nn.sigmoid(value)).astype(BF16)
 
-    load(0).wait()
-    tiled(width // tile, first_hidden)
     corner_on(0)
     own(1).wait()
     complete(0)
     load(2).wait()
 
     def hook_a():
-        in_middle(arrive, 3)
-        at_end(arrive, 2)
-        spread(2)
-
-    tiled(width // tile, first_pre, [(1, hook_a)])
-    some_hidden[z] = hidden[:, units_here]
-    bridge_on(1)
+        spread(1)
+
+    def hook_b():
+        for s in range(1, n_e):
+            j = plane(s)
+            remote(piece.at[j], d_out.at[z, j], o_send.at[0], o_recv.at[j],
+                   at_plane(j)).wait_recv()
+        own(2).wait()
+        for h in range(2):
+            line_out(0, 0, h).start()
+            in_middle(lambda: line_out(0, 1, h).start())
+
+    tiled(width // tile, first_pre, [(1, hook_a), (2, hook_b)])
+    keep(0).start()
+    in_middle(arrive, 3)
+    at_end(arrive, 2)
+    load(0).wait()
 
     def first_output(c):
         value = jnp.dot(hidden[...], later[:, part_of(c)], preferred_element_type=F32)
@@ -658,6 +672,10 @@
     own(3).start()
     for s in range(1, n_e):
         made_out(s).start()
+    spread(2)
+    some_hidden[z] = hidden[:, units_here]
+    tiled(width // tile, later_hidden(0))
+    keep(4).start()
 
     def compute(c):
         value = lax.dot_general(d_pre[z], weights[part_of(c), :], (((1,), (1,)), ((), ())),
@@ -677,27 +695,26 @@
     near_out(0).start()
     compute(1)
     combine(0)
-    corner_on(1)
-
-    def hook_b():
-        line_arrive(1)
-        in_middle(line_arrive, 2)
-
-    def hook_c():
+    bridge_on(1)
+
+    def hook_c(h):
+        def hook():
+            line_arrive(1, h)
+            in_middle(line_arrive, 2, h)
+        return hook
+
+    def hook_d():
         at_end(arrive, 3)
         spread(3)
 
-    def middle_tile(c):
+    hooks = [(2, hook_c(0)), (5, hook_d), (6, hook_c(1)), (7, lambda: corner_on(1))]
+
+    @pl.loop(2, count)
+    def _(c):
         near_out(c - 1).start()
         send(c - 2)
         compute(c)
         combine(c - 1)
-
-    hooks = [(2, hook_b), (3, lambda: bridge_on(2)), (4, hook_c)]
-
-    @pl.loop(2, count)
-    def _(c):
-        middle_tile(c)
         for at, hook in hooks:
             pl.when(c == at)(hook)
 
@@ -706,21 +723,27 @@
     combine(count - 1)
     send(count - 1)
     complete(1)
-    tiled(width // tile, later_pre(1), [(1, lambda: corner_on(2))])
-
-    def hook_d():
-        in_middle(line_arrive, 3)
-        at_end(line_arrive, 2)
-
-    tiled(width // tile, later_hidden(1), [(1, lambda: bridge_on(3))])
+    keep(1).start()
+    tiled(width // tile, later_pre(1), [(0, lambda: bridge_on(2)),
+                                        (2, lambda: in_middle(line_arrive, 3, 0)),
+                                        (3, lambda: corner_on(2))])
     keep_units(1)
+    tiled(width // tile, later_hidden(1), [(2, lambda: bridge_on(3)),
+                                           (3, lambda: in_middle(line_arrive, 3, 1))])
+    keep(5).start()
     complete(2)
-    tiled(width // tile, later_pre(2), [(1, hook_d), (2, lambda: corner_on(3))])
+    keep(2).start()
+    tiled(width // tile, later_pre(2), [(2, lambda: corner_on(3))])
     keep_units(2)
-    tiled(width // tile, later_hidden(2))
     complete(3)
+    keep(3).start()
     tiled(width // tile, later_pre(3))
     keep_units(3)
+    keep(9).start()
+    at_end(line_arrive, 2, 0)
+    at_end(line_arrive, 2, 1)
+    tiled(width // tile, later_hidden(2))
+    keep(6).start()
 
     own(3).wait()
     for s in range(1, n_e):
@@ -748,8 +771,13 @@
             total = total + got[c, k].astype(F32)
         d_trunk[:, part_of(c)] = total.astype(BF16)
 
-    at_end(line_arrive, 3)
+    keep(10).start()
+    keep(11).start()
+    at_end(line_arrive, 3, 0)
+    at_end(line_arrive, 3, 1)
+    keep(8).start()
     tiled(width // tile, later_hidden(3))
+    keep(7).start()
 
     own(4).wait()
     for s in range(1, n_e):
@@ -763,24 +791,31 @@
     for g in range(n_d):
         for k in range(7):
             trunk_out(g, k).wait_send()
+    keep(12).start()
     trunk_out(0, 7).wait_send()
-    line_out(0, 0).wait_send()
+    for h in range(2):
+        line_out(0, 0, h).wait_send()
 
     @pl.when(inner)
     def _():
         trunk_out(0, 8).wait_send()
-        line_out(0, 1).wait_send()
         trunk_out(1, 8).wait_send()
-        line_out(1, 1).wait_send()
         for g in range(2, n_d):
             trunk_out(g, 7).wait_send()
-            line_out(g, 0).wait_send()
+        for h in range(2):
+            line_out(0, 1, h).wait_send()
+            line_out(1, 1, h).wait_send()
+            for g in range(2, n_d):
+                line_out(g, 0, h).wait_send()
 
     @pl.loop(0, count)
     def _(c):
         near_out(c).wait_send()
         for s in range(1, pairs):
             part_out(c, s).wait_send()
+
+    for k in range(13):
+        keep(k).wait()
 
 
 def step_all(trunk, gates, cot, first, second):
@@ -790,74 +825,174 @@
     out = second.shape[1]
     group = n_e * share
     count, pairs, tile = depth // 512, n_e // 2, 512
-    anywhere = pl.BlockSpec(memory_space=pl.ANY)
     hbm = pl.BlockSpec(memory_space=pltpu.HBM)
-    vmem = pl.BlockSpec(memory_space=pltpu.VMEM)
     dma = pltpu.SemaphoreType.DMA
+    gate_shape = (n_e, share, LANES)
     return pl.pallas_call(
         functools.partial(step_kernel, n_e, n_d),
         out_shape=(
-            jax.ShapeDtypeStruct((n_d, n_e, share, depth), BF16),
+            jax.ShapeDtypeStruct((n_d, n_e, share, depth // n_d), BF16),
             jax.ShapeDtypeStruct((n_d, n_e, share, out), BF16),
             jax.ShapeDtypeStruct((n_d, group, width), BF16),
             jax.ShapeDtypeStruct((n_d, group, width // n_d), BF16),
             jax.ShapeDtypeStruct((cot.shape[0], out), BF16),
             jax.ShapeDtypeStruct((share, depth), BF16),
-            jax.ShapeDtypeStruct(gates.shape, F32),
+            jax.ShapeDtypeStruct(gate_shape, F32),
         ),
-        in_specs=[hbm, vmem, hbm, hbm, hbm],
-        out_specs=(vmem,) * 7,
+        in_specs=[hbm] * 5,
+        out_specs=(hbm,) * 7,
         scratch_shapes=[
+            pltpu.VMEM((n_d, n_e, share, depth), BF16),
+            pltpu.VMEM((n_d, n_e, share, out), BF16),
+            pltpu.VMEM((n_d, group, width), BF16),
+            pltpu.VMEM((n_d, group, width // n_d), BF16),
+            pltpu.VMEM((cot.shape[0], out), BF16),
+            pltpu.VMEM((share, depth), BF16),
+            pltpu.VMEM(gate_shape, F32),
+            pltpu.VMEM(gates.shape, BF16),
+            pltpu.VMEM(gate_shape, F32),
             pltpu.VMEM(first.shape, BF16),
             pltpu.VMEM(second.shape, BF16),
             pltpu.VMEM(cot.shape, BF16),
-            pltpu.VMEM(gates.shape, F32),
+            pltpu.VMEM(gate_shape, F32),
             pltpu.VMEM((group, cot.shape[0]), BF16),
             pltpu.VMEM((n_e, share, out), BF16),
             pltpu.VMEM((n_d, group, width), F32),
             pltpu.VMEM((group, width), BF16),
             pltpu.VMEM((n_e, share, out), BF16),
             pltpu.VMEM((n_e, share, out), BF16),
-            pltpu.VMEM(gates.shape, F32),
+            pltpu.VMEM(gate_shape, F32),
             pltpu.VMEM((count, pairs, 2, share, tile), BF16),
             pltpu.VMEM((count, pairs, share, tile), BF16),
             pltpu.VMEM((count, pairs, share, tile), BF16),
             pltpu.VMEM((count, pairs, share, tile), BF16),
-            dma((3,)), dma((5,)),
+            dma((4,)), dma((5,)),
             dma((n_e,)), dma((n_e,)),
             dma((n_d, 9)), dma((n_d, n_e)),
             dma((n_e,)), dma((n_e,)),
-            dma((n_d, 2)), dma((n_d,)),
+            dma((n_d, 2, 2)), dma((n_d, 2)),
             dma((n_e,)), dma((n_e,)),
             dma((count,)), dma((count,)),
             dma((count, pairs)), dma((count, pairs)),
-            dma((n_e,)), dma((n_e,)),
+            dma((n_e,)), dma((n_e,)), dma((13,)),
         ],
         compiler_params=pltpu.CompilerParams(
-            collective_id=2, has_side_effects=True, vmem_limit_bytes=48 * 1024 * 1024),
+            collective_id=2, has_side_effects=True, vmem_limit_bytes=VMEM_BYTES),
     )(trunk, gates, cot, first, second)
 
 
+def finish_kernel(columns, d_pre, units, d_out, mixed, d_trunk, back,
+                  d_first, d_second, mixed_out, d_trunk_out, d_gate,
+                  columns_v, d_pre_v, units_v, d_out_v, mixed_v, d_trunk_v, back_v,
+                  first_v, second_v, gate_v, in_sem, out_sem, tile_sem, wide_sem):
+    pairs = [(units, units_v), (d_out, d_out_v), (columns, columns_v), (mixed, mixed_v),
+             (d_trunk, d_trunk_v), (back, back_v)]
+    steps = d_pre.shape[0]
+
+    def take(k):
+        return pltpu.make_async_copy(*pairs[k], in_sem.at[k])
+
+    def wide(k):
+        return pltpu.make_async_copy(d_pre.at[k], d_pre_v.at[k], wide_sem.at[k])
+
+    def give(k):
+        src, dst = [(second_v, d_second), (mixed_v, mixed_out), (d_trunk_v, d_trunk_out),
+                    (gate_v, d_gate)][k]
+        return pltpu.make_async_copy(src, dst, out_sem.at[k])
+
+    for k in range(3):
+        take(k).start()
+    for k in range(steps):
+        wide(k).start()
+    for k in range(3, len(pairs)):
+        take(k).start()
+    take(0).wait()
+    take(1).wait()
+    second_v[...] = lax.dot_general(
+        units_v[...], d_out_v[...], (((0,), (0,)), ((), ())),
+        preferred_element_type=F32).astype(BF16)
+    give(0).start()
+    take(2).wait()
+    for k in range(steps):
+        wide(k).wait()
+    tile = first_v.shape[1]
+    count = first_v.shape[0]
+
+    def store(c):
+        here = pl.ds(pl.multiple_of(c * tile, tile), tile)
+        return pltpu.make_async_copy(first_v.at[c], d_first.at[here], tile_sem.at[c])
+
+    @pl.loop(0, count)
+    def _(c):
+        here = pl.ds(pl.multiple_of(c * tile, tile), tile)
+        right = d_pre_v[...].reshape(-1, d_pre_v.shape[2])
+        first_v[c] = lax.dot_general(
+            columns_v[:, here], right, (((0,), (0,)), ((), ())),
+            preferred_element_type=F32).astype(BF16)
+        store(c).start()
+
+        @pl.when(c == 0)
+        def _():
+            take(3).wait()
+            give(1).start()
+            take(4).wait()
+            give(2).start()
+            take(5).wait()
+            tasks = d_gate.shape[0]
+            eye = jnp.where(
+                lax.broadcasted_iota(jnp.int32, (tasks, LANES), 0)
+                == lax.broadcasted_iota(jnp.int32, (tasks, LANES), 1), 1.0, 0.0).astype(BF16)
+            gate_v[...] = lax.dot_general(
+                eye, back_v[...].astype(BF16), (((1,), (1,)), ((), ())),
+                preferred_element_type=F32).astype(BF16)
+            give(3).start()
+
+    for k in range(4):
+        give(k).wait()
+
+    @pl.loop(0, count)
+    def _(c):
+        store(c).wait()
+
+
+def finish_all(columns, d_pre, units, d_out, mixed, d_trunk, back, tasks):
+    hbm = pl.BlockSpec(memory_space=pltpu.HBM)
+    dma = pltpu.SemaphoreType.DMA
+    rows, depth = columns.shape
+    steps, group, width = d_pre.shape
+    unit, out = units.shape[1], d_out.shape[1]
+    tile = 256
+    ins = (columns, d_pre, units, d_out, mixed, d_trunk, back)
+    return pl.pallas_call(
+        finish_kernel,
+        out_shape=(
+            jax.ShapeDtypeStruct((depth, width), BF16),
+            jax.ShapeDtypeStruct((unit, out), BF16),
+            jax.ShapeDtypeStruct(mixed.shape, BF16),
+            jax.ShapeDtypeStruct(d_trunk.shape, BF16),
+            jax.ShapeDtypeStruct((tasks, back.shape[0]), BF16),
+        ),
+        in_specs=[hbm] * 7,
+        out_specs=(hbm,) * 5,
+        scratch_shapes=[pltpu.VMEM(x.shape, x.dtype) for x in ins] + [
+            pltpu.VMEM((depth // tile, tile, width), BF16),
+            pltpu.VMEM((unit, out), BF16),
+            pltpu.VMEM((tasks, back.shape[0]), BF16),
+            dma((6,)), dma((4,)), dma((depth // tile,)), dma((steps,)),
+        ],
+        compiler_params=pltpu.CompilerParams(vmem_limit_bytes=VMEM_BYTES),
+    )(*ins)
+
+
 def on_square(trunk, w_first, w_second, gates, d_mixed):
-    rank = lax.axis_index("dp")
-    n_e, n_d = lax.axis_size("expert"), lax.axis_size("dp")
     first, second, gate_here = w_first[0], w_second[0], gates[0]
     tasks, group = gate_here.shape
-    share = group // n_e
-    depth = first.shape[0] // n_d
-    gate_parts = jnp.pad(gate_here.T.astype(F32).reshape(n_e, share, tasks),
-                         ((0, 0), (0, 0), (0, LANES - tasks)))
-    rows, d_out, d_pre, some_hidden, mixed, d_trunk, back = step_all(
-        trunk, gate_parts, d_mixed.reshape(share * tasks, -1), first, second)
-    d_gate = back[:, :, :tasks].reshape(group, tasks).T.astype(BF16)[None]
-    columns = lax.dynamic_slice_in_dim(rows.reshape(-1, first.shape[0]), rank * depth, depth, 1)
-    d_first = lax.dot_general(
-        columns, d_pre.reshape(-1, first.shape[1]), (((0,), (0,)), ((), ())),
-        preferred_element_type=F32).astype(BF16)
-    d_second = lax.dot_general(
-        some_hidden.reshape(-1, some_hidden.shape[2]), d_out.reshape(-1, second.shape[1]),
-        (((0,), (0,)), ((), ())), preferred_element_type=F32).astype(BF16)
-    return (mixed.reshape(d_mixed.shape), d_trunk, d_gate, d_first[None], d_second[None])
+    columns, d_out, d_pre, units, mixed, d_trunk, back = step_all(
+        trunk, gate_here, d_mixed.reshape(-1, d_mixed.shape[2]), first, second)
+    d_first, d_second, mixed, d_trunk, d_gate = finish_all(
+        columns.reshape(-1, columns.shape[3]), d_pre, units.reshape(-1, units.shape[2]),
+        d_out.reshape(-1, d_out.shape[3]), mixed, d_trunk, back.reshape(group, -1), tasks)
+    return (mixed.reshape(d_mixed.shape), d_trunk, d_gate[None], d_first[None], d_second[None])
 
 
 def solution(mesh):

time: 83.9 us -> 83.5 us (level)
  Pallas kernels: 69.7 us -> 82.6 us
  matrix products: 8.45 us -> 0 us
  local copies, waits for them, and re-layouts: 4.84 us -> 0 us
    pallas_call x0 -> x1, Pallas kernels: none -> 8.61 us  [finish_all(): pl.pallas_call(finish_kernel, out_shape=(jax.ShapeDtypeStruct((depth, wid...]
    dot_general x2 -> x0, matrix products: 8.45 us -> none  [the longest x1 6.48 us: on_square(): lax.dot_general(columns, d_pre.reshape(-1, first.shape[1]), (((0,), (0,))...]
    pallas_call x1, Pallas kernels: 69.7 us -> 74 us  [step_all(): pl.pallas_call(functools.partial(step_kernel, n_e, n_d), out_shape=(jax.S...]
    unnamed x8 -> x0, local copies, waits for them, and re-layouts: 3.34 us -> none
    convert_element_type x2 -> x0, local copies, waits for them, and re-layouts: 1.49 us -> none  [the longest x1 0.81 us: on_square(): gate_here.T.astype(F32).reshape(n_e, share, tasks)]
where the time goes in v2:
time: 83.5 us; the launch traced here: 83.3 us
  Pallas kernels  82.6 us (99%)
    pallas_call x1, Pallas kernels, step_all(): pl.pallas_call(functools.partial(step_kernel, n_e, n_d), out_shape=(jax.S...  74 us
    pallas_call x1, Pallas kernels, finish_all(): pl.pallas_call(finish_kernel, out_shape=(jax.ShapeDtypeStruct((depth, wid...  8.61 us

profile of v2, /device:TPU:0, one launch (start us, length us, event | category | flops | bytes accessed | tf_op | source)
XLA Modules:
  0.0 83.3 jit_solution(8773756699349549476)
XLA Ops:
  0.6 74.0 %shard_map.92 = (bf16[4,8,24,1024]{3,2,1,0:T(8,128)(2,1)}, bf16[4,8,24,1024]{3,2,1,0:T(8,128)(2,1)}, bf16[4,192,2048]{2,1,0:T(8,128)(2,1)}, bf16[4,192,512]{2,1,...) custom-call(bf16[24,4096]{1,0:T(8,128)(2,1)} %trunk.1, ...), custom_call_target="tpu_custom_call" | custom-call | tf_op jit(solution)/shard_map/pallas_call | solution.py:831
  74.7 8.6 %shard_map.93 = (bf16[1024,2048]{1,0:T(8,128)(2,1)}, bf16[512,1024]{1,0:T(8,128)(2,1)}, bf16[192,1024]{1,0:T(8,128)(2,1)}, bf16[24,4096]{1,0:T(8,128)(2,1)}, bf16[8,192]{1,0:T(8,128)(2,1)}) custom-call(bf16[768,1024]{1,0:T(8,128)(2,1)} %bitcast.14, bf16[4,192,2048]{2,1,0:T(8,128)(2,1)} %get-tuple-element.18.d_pre, bf16[768,512]{1,0:T(8,128)(2,1)} %bitcast.16, ...), custom_call_target="tpu_custom_call" | custom-call | tf_op jit(solution)/shard_map/pallas_call | solution.py:966

commit v3 on v2

--- a/solution.py
+++ b/solution.py
@@ -403,7 +403,7 @@
 def step_kernel(n_e, n_d, trunk, gates, cot_in, first, second,
                 columns_out, d_out_out, d_pre_out, units_out, mixed_out, d_trunk_out, back_out_ref,
                 rows, d_out, d_pre, some_hidden, mixed, d_trunk, gate_back, gate_in, gate_piece,
-                weights, later, cot, gate_each, mix, piece, tall, hidden, made, outs, d_gate,
+                weights, later, turned, cot, gate_each, mix, piece, tall, hidden, made, outs, d_gate,
                 part, near, pair, got,
                 load_sem, own_sem, g_send, g_recv, t_send, t_recv, o_send, o_recv, z_send, z_recv,
                 m_send, m_recv, n_send, n_recv, p_send, p_recv, b_send, b_recv, out_sem):
@@ -570,6 +570,16 @@
     pl.when(inner)(lambda: trunk_out(0, 8).start())
     spread(0)
 
+    def turn(low, high):
+        @pl.loop(low, high)
+        def _(c):
+            here = pl.ds(pl.multiple_of(c * 256, 256), 256)
+            turned[:, here] = later[here, :].T
+
+    turns = width // 256
+    load(0).wait()
+    turn(0, turns // 2)
+
     def task_of():
         shape = (LANES, share * tasks)
         return jnp.where(
@@ -593,12 +603,21 @@
                 * same_sample()).astype(BF16)
     piece[...] = jnp.dot(mix[...], cot[...], preferred_element_type=F32).astype(BF16).reshape(
         piece.shape)
-    bridge_on(0)
     for s in range(1, n_e):
         piece_out(s).start()
     own(2).start()
+
+    turn(turns // 2, turns)
+    bridge_on(0)
     arrive(1)
     in_middle(arrive, 2)
+    for s in range(1, n_e):
+        j = plane(s)
+        remote(piece.at[j], d_out.at[z, j], o_send.at[0], o_recv.at[j], at_plane(j)).wait_recv()
+    own(2).wait()
+    for h in range(2):
+        line_out(0, 0, h).start()
+        in_middle(lambda: line_out(0, 1, h).start())
 
     tile = 512
 
@@ -607,8 +626,7 @@
 
     def back_hidden(g, c):
         left = d_out[order[g]].reshape(group, d_out.shape[3])
-        return lax.dot_general(left, later[part_of(c), :], (((1,), (1,)), ((), ())),
-                               preferred_element_type=F32)
+        return jnp.dot(left, turned[:, part_of(c)], preferred_element_type=F32)
 
     def forward_pre(g, c):
         left = rows[order[g]].reshape(group, depth)
@@ -619,9 +637,12 @@
         d_pre[order[g], :, part_of(c)] = (
             d_hidden * sig * (1.0 + value * (1.0 - sig))).astype(BF16)
 
+    def first_hidden(c):
+        tall[0, :, part_of(c)] = back_hidden(0, c)
+
     def first_pre(c):
         value = forward_pre(0, c)
-        tall[0, :, part_of(c)] = value
+        store_d_pre(0, c, tall[0, :, part_of(c)], value)
         hidden[:, part_of(c)] = (value * jax.nn.sigmoid(value)).astype(BF16)
 
     def later_pre(g):
@@ -640,29 +661,22 @@
         value = tall[g, :, units_here]
         some_hidden[order[g]] = (value * jax.nn.sigmoid(value)).astype(BF16)
 
+    tiled(width // tile, first_hidden)
+    spread(1)
     corner_on(0)
     own(1).wait()
     complete(0)
     load(2).wait()
 
     def hook_a():
-        spread(1)
-
-    def hook_b():
-        for s in range(1, n_e):
-            j = plane(s)
-            remote(piece.at[j], d_out.at[z, j], o_send.at[0], o_recv.at[j],
-                   at_plane(j)).wait_recv()
-        own(2).wait()
-        for h in range(2):
-            line_out(0, 0, h).start()
-            in_middle(lambda: line_out(0, 1, h).start())
-
-    tiled(width // tile, first_pre, [(1, hook_a), (2, hook_b)])
+        in_middle(arrive, 3)
+        at_end(arrive, 2)
+        spread(2)
+
+    tiled(width // tile, first_pre, [(2, hook_a)])
     keep(0).start()
-    in_middle(arrive, 3)
-    at_end(arrive, 2)
-    load(0).wait()
+    keep(4).start()
+    some_hidden[z] = hidden[:, units_here]
 
     def first_output(c):
         value = jnp.dot(hidden[...], later[:, part_of(c)], preferred_element_type=F32)
@@ -670,12 +684,7 @@
 
     tiled(made.shape[2] // tile, first_output)
     own(3).start()
-    for s in range(1, n_e):
-        made_out(s).start()
-    spread(2)
-    some_hidden[z] = hidden[:, units_here]
-    tiled(width // tile, later_hidden(0))
-    keep(4).start()
+    bridge_on(1)
 
     def compute(c):
         value = lax.dot_general(d_pre[z], weights[part_of(c), :], (((1,), (1,)), ((), ())),
@@ -686,64 +695,70 @@
         near_out(c).wait_recv()
         pair[c] = (part[c, :, core].astype(F32) + near[c].astype(F32)).astype(BF16)
 
-    def send(c):
-        for s in range(1, pairs):
-            part_out(c, s).start()
+    def send_parts(low, high):
+        @pl.loop(low, high)
+        def _(c):
+            for s in range(1, pairs):
+                part_out(c, s).start()
 
     count = depth // tile
     compute(0)
     near_out(0).start()
     compute(1)
     combine(0)
-    bridge_on(1)
-
-    def hook_c(h):
-        def hook():
+
+    def hook_b():
+        at_end(arrive, 3)
+        at_end(spread, 3)
+
+    def hook_c():
+        for h in range(2):
             line_arrive(1, h)
             in_middle(line_arrive, 2, h)
-        return hook
-
-    def hook_d():
-        at_end(arrive, 3)
-        spread(3)
-
-    hooks = [(2, hook_c(0)), (5, hook_d), (6, hook_c(1)), (7, lambda: corner_on(1))]
+
+    hooks = [(2, lambda: in_middle(spread, 3)), (4, hook_b), (5, lambda: bridge_on(2)),
+             (6, hook_c), (7, lambda: corner_on(1))]
 
     @pl.loop(2, count)
     def _(c):
         near_out(c - 1).start()
-        send(c - 2)
         compute(c)
         combine(c - 1)
         for at, hook in hooks:
             pl.when(c == at)(hook)
 
     near_out(count - 1).start()
-    send(count - 2)
-    combine(count - 1)
-    send(count - 1)
     complete(1)
     keep(1).start()
-    tiled(width // tile, later_pre(1), [(0, lambda: bridge_on(2)),
-                                        (2, lambda: in_middle(line_arrive, 3, 0)),
-                                        (3, lambda: corner_on(2))])
+    tiled(width // tile, later_pre(1), [(0, lambda: combine(count - 1)),
+                                        (2, lambda: bridge_on(3))])
     keep_units(1)
-    tiled(width // tile, later_hidden(1), [(2, lambda: bridge_on(3)),
-                                           (3, lambda: in_middle(line_arrive, 3, 1))])
+    send_parts(0, count // 2)
+    tiled(width // tile, later_hidden(1), [(1, lambda: corner_on(2))])
+    send_parts(count // 2, count)
     keep(5).start()
     complete(2)
     keep(2).start()
-    tiled(width // tile, later_pre(2), [(2, lambda: corner_on(3))])
+
+    def hook_d():
+        for h in range(2):
+            in_middle(line_arrive, 3, h)
+
+    def hook_e():
+        for s in range(1, n_e):
+            made_out(s).start()
+
+    tiled(width // tile, later_pre(2), [(0, hook_e), (1, hook_d), (3, lambda: corner_on(3))])
     keep_units(2)
+    for h in range(2):
+        at_end(line_arrive, 2, h)
+    tiled(width // tile, later_hidden(2))
+    keep(6).start()
     complete(3)
     keep(3).start()
     tiled(width // tile, later_pre(3))
     keep_units(3)
     keep(9).start()
-    at_end(line_arrive, 2, 0)
-    at_end(line_arrive, 2, 1)
-    tiled(width // tile, later_hidden(2))
-    keep(6).start()
 
     own(3).wait()
     for s in range(1, n_e):
@@ -853,6 +868,7 @@
             pltpu.VMEM(gate_shape, F32),
             pltpu.VMEM(first.shape, BF16),
             pltpu.VMEM(second.shape, BF16),
+            pltpu.VMEM(second.shape[::-1], BF16),
             pltpu.VMEM(cot.shape, BF16),
             pltpu.VMEM(gate_shape, F32),
             pltpu.VMEM((group, cot.shape[0]), BF16),

time: 83.5 us -> 73.9 us (0.89)
  Pallas kernels: 82.6 us -> 73.1 us
    pallas_call x1, Pallas kernels: 74 us -> 64.5 us  [step_all(): pl.pallas_call(functools.partial(step_kernel, n_e, n_d), out_shape=(jax.S...]
where the time goes in v3:
time: 73.9 us; the launch traced here: 73.8 us
  Pallas kernels  73.1 us (99%)
    pallas_call x1, Pallas kernels, step_all(): pl.pallas_call(functools.partial(step_kernel, n_e, n_d), out_shape=(jax.S...  64.5 us
    pallas_call x1, Pallas kernels, finish_all(): pl.pallas_call(finish_kernel, out_shape=(jax.ShapeDtypeStruct((depth, wid...  8.61 us

profile of v3, /device:TPU:0, one launch (start us, length us, event | category | flops | bytes accessed | tf_op | source)
XLA Modules:
  0.0 73.8 jit_solution(13603434067405838193)
XLA Ops:
  0.6 64.5 %shard_map.92 = (bf16[4,8,24,1024]{3,2,1,0:T(8,128)(2,1)}, bf16[4,8,24,1024]{3,2,1,0:T(8,128)(2,1)}, bf16[4,192,2048]{2,1,0:T(8,128)(2,1)}, bf16[4,192,512]{2,1,...) custom-call(bf16[24,4096]{1,0:T(8,128)(2,1)} %trunk.1, ...), custom_call_target="tpu_custom_call" | custom-call | tf_op jit(solution)/shard_map/pallas_call | solution.py:846
  65.1 8.6 %shard_map.93 = (bf16[1024,2048]{1,0:T(8,128)(2,1)}, bf16[512,1024]{1,0:T(8,128)(2,1)}, bf16[192,1024]{1,0:T(8,128)(2,1)}, bf16[24,4096]{1,0:T(8,128)(2,1)}, bf16[8,192]{1,0:T(8,128)(2,1)}) custom-call(bf16[768,1024]{1,0:T(8,128)(2,1)} %bitcast.14, bf16[4,192,2048]{2,1,0:T(8,128)(2,1)} %get-tuple-element.18.d_pre, bf16[768,512]{1,0:T(8,128)(2,1)} %bitcast.16, ...), custom_call_target="tpu_custom_call" | custom-call | tf_op jit(solution)/shard_map/pallas_call | solution.py:982

commit v4 on v3

--- a/solution.py
+++ b/solution.py
@@ -621,33 +621,35 @@
 
     tile = 512
 
-    def part_of(c):
-        return pl.ds(pl.multiple_of(c * tile, tile), tile)
-
-    def back_hidden(g, c):
+    broad = 2 * tile
+
+    def part_of(c, span=tile):
+        return pl.ds(pl.multiple_of(c * span, span), span)
+
+    def back_hidden(g, c, span=tile):
         left = d_out[order[g]].reshape(group, d_out.shape[3])
-        return jnp.dot(left, turned[:, part_of(c)], preferred_element_type=F32)
-
-    def forward_pre(g, c):
+        return jnp.dot(left, turned[:, part_of(c, span)], preferred_element_type=F32)
+
+    def forward_pre(g, c, span=tile):
         left = rows[order[g]].reshape(group, depth)
-        return jnp.dot(left, weights[:, part_of(c)], preferred_element_type=F32)
-
-    def store_d_pre(g, c, d_hidden, value):
+        return jnp.dot(left, weights[:, part_of(c, span)], preferred_element_type=F32)
+
+    def store_d_pre(g, c, d_hidden, value, span=tile):
         sig = jax.nn.sigmoid(value)
-        d_pre[order[g], :, part_of(c)] = (
+        d_pre[order[g], :, part_of(c, span)] = (
             d_hidden * sig * (1.0 + value * (1.0 - sig))).astype(BF16)
 
     def first_hidden(c):
-        tall[0, :, part_of(c)] = back_hidden(0, c)
+        tall[0, :, part_of(c, broad)] = back_hidden(0, c, broad)
 
     def first_pre(c):
         value = forward_pre(0, c)
         store_d_pre(0, c, tall[0, :, part_of(c)], value)
         hidden[:, part_of(c)] = (value * jax.nn.sigmoid(value)).astype(BF16)
 
-    def later_pre(g):
+    def later_pre(g, span=tile):
         def body(c):
-            tall[g, :, part_of(c)] = forward_pre(g, c)
+            tall[g, :, part_of(c, span)] = forward_pre(g, c, span)
         return body
 
     def later_hidden(g):
@@ -661,15 +663,15 @@
         value = tall[g, :, units_here]
         some_hidden[order[g]] = (value * jax.nn.sigmoid(value)).astype(BF16)
 
-    tiled(width // tile, first_hidden)
+    tiled(width // broad, first_hidden)
     spread(1)
     corner_on(0)
+    in_middle(arrive, 3)
     own(1).wait()
     complete(0)
     load(2).wait()
 
     def hook_a():
-        in_middle(arrive, 3)
         at_end(arrive, 2)
         spread(2)
 
@@ -678,13 +680,6 @@
     keep(4).start()
     some_hidden[z] = hidden[:, units_here]
 
-    def first_output(c):
-        value = jnp.dot(hidden[...], later[:, part_of(c)], preferred_element_type=F32)
-        made[:, :, part_of(c)] = value.astype(BF16).reshape(n_e, share, tile)
-
-    tiled(made.shape[2] // tile, first_output)
-    own(3).start()
-    bridge_on(1)
 
     def compute(c):
         value = lax.dot_general(d_pre[z], weights[part_of(c), :], (((1,), (1,)), ((), ())),
@@ -704,6 +699,7 @@
     count = depth // tile
     compute(0)
     near_out(0).start()
+    bridge_on(1)
     compute(1)
     combine(0)
 
@@ -716,8 +712,8 @@
             line_arrive(1, h)
             in_middle(line_arrive, 2, h)
 
-    hooks = [(2, lambda: in_middle(spread, 3)), (4, hook_b), (5, lambda: bridge_on(2)),
-             (6, hook_c), (7, lambda: corner_on(1))]
+    hooks = [(2, lambda: in_middle(spread, 3)), (4, hook_b), (6, lambda: bridge_on(2)),
+             (7, lambda: corner_on(1))]
 
     @pl.loop(2, count)
     def _(c):
@@ -728,14 +724,20 @@
             pl.when(c == at)(hook)
 
     near_out(count - 1).start()
+
+    def first_output(c):
+        value = jnp.dot(hidden[...], later[:, part_of(c)], preferred_element_type=F32)
+        made[:, :, part_of(c)] = value.astype(BF16).reshape(n_e, share, tile)
+
+    tiled(made.shape[2] // tile, first_output)
+    own(3).start()
     complete(1)
     keep(1).start()
-    tiled(width // tile, later_pre(1), [(0, lambda: combine(count - 1)),
+    tiled(width // tile, later_pre(1), [(0, lambda: combine(count - 1)), (1, hook_c),
                                         (2, lambda: bridge_on(3))])
     keep_units(1)
+    tiled(width // tile, later_hidden(1), [(1, lambda: corner_on(2))])
     send_parts(0, count // 2)
-    tiled(width // tile, later_hidden(1), [(1, lambda: corner_on(2))])
-    send_parts(count // 2, count)
     keep(5).start()
     complete(2)
     keep(2).start()
@@ -748,15 +750,17 @@
         for s in range(1, n_e):
             made_out(s).start()
 
-    tiled(width // tile, later_pre(2), [(0, hook_e), (1, hook_d), (3, lambda: corner_on(3))])
+    tiled(width // tile, later_pre(2), [(2, hook_e)])
+    hook_d()
     keep_units(2)
+    send_parts(count // 2, count)
     for h in range(2):
         at_end(line_arrive, 2, h)
-    tiled(width // tile, later_hidden(2))
+    tiled(width // tile, later_hidden(2), [(1, lambda: corner_on(3))])
     keep(6).start()
     complete(3)
     keep(3).start()
-    tiled(width // tile, later_pre(3))
+    tiled(width // broad, later_pre(3, broad))
     keep_units(3)
     keep(9).start()
 
@@ -775,6 +779,13 @@
         back_out(s).start()
     mixed[...] = lax.dot_general(mix[...], each_out, (((0,), (0,)), ((), ())),
                                  preferred_element_type=F32).astype(BF16)
+
+    keep(10).start()
+    at_end(line_arrive, 3, 0)
+    at_end(line_arrive, 3, 1)
+    keep(8).start()
+    tiled(width // tile, later_hidden(3))
+    keep(7).start()
 
     @pl.loop(0, count)
     def _(c):
@@ -786,13 +797,7 @@
             total = total + got[c, k].astype(F32)
         d_trunk[:, part_of(c)] = total.astype(BF16)
 
-    keep(10).start()
     keep(11).start()
-    at_end(line_arrive, 3, 0)
-    at_end(line_arrive, 3, 1)
-    keep(8).start()
-    tiled(width // tile, later_hidden(3))
-    keep(7).start()
 
     own(4).wait()
     for s in range(1, n_e):

time: 73.9 us -> 71.4 us (0.966)
  Pallas kernels: 73.1 us -> 70.6 us
    pallas_call x1, Pallas kernels: 64.5 us -> 62 us  [step_all(): pl.pallas_call(functools.partial(step_kernel, n_e, n_d), out_shape=(jax.S...]
where the time goes in v4:
time: 71.4 us; the launch traced here: 71.2 us
  Pallas kernels  70.6 us (99%)
    pallas_call x1, Pallas kernels, step_all(): pl.pallas_call(functools.partial(step_kernel, n_e, n_d), out_shape=(jax.S...  62 us
    pallas_call x1, Pallas kernels, finish_all(): pl.pallas_call(finish_kernel, out_shape=(jax.ShapeDtypeStruct((depth, wid...  8.61 us

profile of v4, /device:TPU:0, one launch (start us, length us, event | category | flops | bytes accessed | tf_op | source)
XLA Modules:
  0.0 71.2 jit_solution(2042982564416552980)
XLA Ops:
  0.6 62.0 %shard_map.92 = (bf16[4,8,24,1024]{3,2,1,0:T(8,128)(2,1)}, bf16[4,8,24,1024]{3,2,1,0:T(8,128)(2,1)}, bf16[4,192,2048]{2,1,0:T(8,128)(2,1)}, bf16[4,192,512]{2,1,...) custom-call(bf16[24,4096]{1,0:T(8,128)(2,1)} %trunk.1, ...), custom_call_target="tpu_custom_call" | custom-call | tf_op jit(solution)/shard_map/pallas_call | solution.py:851
  62.6 8.6 %shard_map.93 = (bf16[1024,2048]{1,0:T(8,128)(2,1)}, bf16[512,1024]{1,0:T(8,128)(2,1)}, bf16[192,1024]{1,0:T(8,128)(2,1)}, bf16[24,4096]{1,0:T(8,128)(2,1)}, bf16[8,192]{1,0:T(8,128)(2,1)}) custom-call(bf16[768,1024]{1,0:T(8,128)(2,1)} %bitcast.14, bf16[4,192,2048]{2,1,0:T(8,128)(2,1)} %get-tuple-element.18.d_pre, bf16[768,512]{1,0:T(8,128)(2,1)} %bitcast.16, ...), custom_call_target="tpu_custom_call" | custom-call | tf_op jit(solution)/shard_map/pallas_call | solution.py:987

commit v5 on v4

--- a/solution.py
+++ b/solution.py
@@ -701,7 +701,6 @@
     near_out(0).start()
     bridge_on(1)
     compute(1)
-    combine(0)
 
     def hook_b():
         at_end(arrive, 3)
@@ -709,17 +708,17 @@
 
     def hook_c():
         for h in range(2):
-            line_arrive(1, h)
+            in_middle(line_arrive, 1, h)
             in_middle(line_arrive, 2, h)
 
-    hooks = [(2, lambda: in_middle(spread, 3)), (4, hook_b), (6, lambda: bridge_on(2)),
+    hooks = [(2, lambda: in_middle(spread, 3)), (4, hook_b), (5, hook_c), (6, lambda: bridge_on(2)),
              (7, lambda: corner_on(1))]
 
     @pl.loop(2, count)
     def _(c):
         near_out(c - 1).start()
         compute(c)
-        combine(c - 1)
+        combine(c - 2)
         for at, hook in hooks:
             pl.when(c == at)(hook)
 
@@ -733,9 +732,16 @@
     own(3).start()
     complete(1)
     keep(1).start()
-    tiled(width // tile, later_pre(1), [(0, lambda: combine(count - 1)), (1, hook_c),
-                                        (2, lambda: bridge_on(3))])
+
+    def hook_f():
+        combine(count - 2)
+        combine(count - 1)
+        bridge_on(3)
+
+    tiled(width // broad, later_pre(1, broad), [(0, hook_f)])
     keep_units(1)
+    for h in range(2):
+        at_end(line_arrive, 1, h)
     tiled(width // tile, later_hidden(1), [(1, lambda: corner_on(2))])
     send_parts(0, count // 2)
     keep(5).start()
@@ -750,8 +756,7 @@
         for s in range(1, n_e):
             made_out(s).start()
 
-    tiled(width // tile, later_pre(2), [(2, hook_e)])
-    hook_d()
+    tiled(width // broad, later_pre(2, broad), [(0, hook_d), (1, hook_e)])
     keep_units(2)
     send_parts(count // 2, count)
     for h in range(2):

time: 71.4 us -> 70 us (0.980)
  Pallas kernels: 70.6 us -> 69.2 us
    pallas_call x1, Pallas kernels: 62 us -> 60.6 us  [step_all(): pl.pallas_call(functools.partial(step_kernel, n_e, n_d), out_shape=(jax.S...]
where the time goes in v5:
time: 70 us; the launch traced here: 69.9 us
  Pallas kernels  69.2 us (99%)
    pallas_call x1, Pallas kernels, step_all(): pl.pallas_call(functools.partial(step_kernel, n_e, n_d), out_shape=(jax.S...  60.6 us
    pallas_call x1, Pallas kernels, finish_all(): pl.pallas_call(finish_kernel, out_shape=(jax.ShapeDtypeStruct((depth, wid...  8.61 us

profile of v5, /device:TPU:0, one launch (start us, length us, event | category | flops | bytes accessed | tf_op | source)
XLA Modules:
  0.0 69.9 jit_solution(10690312414504782243)
XLA Ops:
  0.6 60.6 %shard_map.92 = (bf16[4,8,24,1024]{3,2,1,0:T(8,128)(2,1)}, bf16[4,8,24,1024]{3,2,1,0:T(8,128)(2,1)}, bf16[4,192,2048]{2,1,0:T(8,128)(2,1)}, bf16[4,192,512]{2,1,...) custom-call(bf16[24,4096]{1,0:T(8,128)(2,1)} %trunk.1, ...), custom_call_target="tpu_custom_call" | custom-call | tf_op jit(solution)/shard_map/pallas_call | solution.py:856
  61.3 8.6 %shard_map.93 = (bf16[1024,2048]{1,0:T(8,128)(2,1)}, bf16[512,1024]{1,0:T(8,128)(2,1)}, bf16[192,1024]{1,0:T(8,128)(2,1)}, bf16[24,4096]{1,0:T(8,128)(2,1)}, bf16[8,192]{1,0:T(8,128)(2,1)}) custom-call(bf16[768,1024]{1,0:T(8,128)(2,1)} %bitcast.14, bf16[4,192,2048]{2,1,0:T(8,128)(2,1)} %get-tuple-element.18.d_pre, bf16[768,512]{1,0:T(8,128)(2,1)} %bitcast.16, ...), custom_call_target="tpu_custom_call" | custom-call | tf_op jit(solution)/shard_map/pallas_call | solution.py:992

commit v6 on v5

--- a/solution.py
+++ b/solution.py
@@ -401,7 +401,8 @@
 
 
 def step_kernel(n_e, n_d, trunk, gates, cot_in, first, second,
-                columns_out, d_out_out, d_pre_out, units_out, mixed_out, d_trunk_out, back_out_ref,
+                columns_out, d_pre_out, second_out, mixed_out, d_trunk_out, back_out_ref,
+                d_second,
                 rows, d_out, d_pre, some_hidden, mixed, d_trunk, gate_back, gate_in, gate_piece,
                 weights, later, turned, cot, gate_each, mix, piece, tall, hidden, made, outs, d_gate,
                 part, near, pair, got,
@@ -486,7 +487,7 @@
     def keep(k):
         src, dst = ([(rows.at[zi, :, :, depth_here], columns_out.at[zi]) for zi in order]
                     + [(d_pre.at[zi], d_pre_out.at[zi]) for zi in order]
-                    + [(d_out, d_out_out), (some_hidden, units_out), (mixed, mixed_out),
+                    + [(d_second, second_out), (mixed, mixed_out),
                        (d_trunk, d_trunk_out), (gate_back, back_out_ref)])[k]
         return pltpu.make_async_copy(src, dst, out_sem.at[k])
 
@@ -767,7 +768,6 @@
     keep(3).start()
     tiled(width // broad, later_pre(3, broad))
     keep_units(3)
-    keep(9).start()
 
     own(3).wait()
     for s in range(1, n_e):
@@ -785,12 +785,15 @@
     mixed[...] = lax.dot_general(mix[...], each_out, (((0,), (0,)), ((), ())),
                                  preferred_element_type=F32).astype(BF16)
 
-    keep(10).start()
+    keep(9).start()
     at_end(line_arrive, 3, 0)
     at_end(line_arrive, 3, 1)
-    keep(8).start()
     tiled(width // tile, later_hidden(3))
     keep(7).start()
+    d_second[...] = lax.dot_general(
+        some_hidden[...].reshape(-1, units), d_out[...].reshape(-1, d_out.shape[3]),
+        (((0,), (0,)), ((), ())), preferred_element_type=F32).astype(BF16)
+    keep(8).start()
 
     @pl.loop(0, count)
     def _(c):
@@ -802,7 +805,7 @@
             total = total + got[c, k].astype(F32)
         d_trunk[:, part_of(c)] = total.astype(BF16)
 
-    keep(11).start()
+    keep(10).start()
 
     own(4).wait()
     for s in range(1, n_e):
@@ -816,7 +819,7 @@
     for g in range(n_d):
         for k in range(7):
             trunk_out(g, k).wait_send()
-    keep(12).start()
+    keep(11).start()
     trunk_out(0, 7).wait_send()
     for h in range(2):
         line_out(0, 0, h).wait_send()
@@ -839,7 +842,7 @@
         for s in range(1, pairs):
             part_out(c, s).wait_send()
 
-    for k in range(13):
+    for k in range(12):
         keep(k).wait()
 
 
@@ -857,16 +860,16 @@
         functools.partial(step_kernel, n_e, n_d),
         out_shape=(
             jax.ShapeDtypeStruct((n_d, n_e, share, depth // n_d), BF16),
-            jax.ShapeDtypeStruct((n_d, n_e, share, out), BF16),
             jax.ShapeDtypeStruct((n_d, group, width), BF16),
-            jax.ShapeDtypeStruct((n_d, group, width // n_d), BF16),
+            jax.ShapeDtypeStruct((width // n_d, out), BF16),
             jax.ShapeDtypeStruct((cot.shape[0], out), BF16),
             jax.ShapeDtypeStruct((share, depth), BF16),
             jax.ShapeDtypeStruct(gate_shape, F32),
         ),
         in_specs=[hbm] * 5,
-        out_specs=(hbm,) * 7,
+        out_specs=(hbm,) * 6,
         scratch_shapes=[
+            pltpu.VMEM((width // n_d, out), BF16),
             pltpu.VMEM((n_d, n_e, share, depth), BF16),
             pltpu.VMEM((n_d, n_e, share, out), BF16),
             pltpu.VMEM((n_d, group, width), BF16),
@@ -900,18 +903,18 @@
             dma((n_e,)), dma((n_e,)),
             dma((count,)), dma((count,)),
             dma((count, pairs)), dma((count, pairs)),
-            dma((n_e,)), dma((n_e,)), dma((13,)),
+            dma((n_e,)), dma((n_e,)), dma((12,)),
         ],
         compiler_params=pltpu.CompilerParams(
             collective_id=2, has_side_effects=True, vmem_limit_bytes=VMEM_BYTES),
     )(trunk, gates, cot, first, second)
 
 
-def finish_kernel(columns, d_pre, units, d_out, mixed, d_trunk, back,
+def finish_kernel(columns, d_pre, second, mixed, d_trunk, back,
                   d_first, d_second, mixed_out, d_trunk_out, d_gate,
-                  columns_v, d_pre_v, units_v, d_out_v, mixed_v, d_trunk_v, back_v,
-                  first_v, second_v, gate_v, in_sem, out_sem, tile_sem, wide_sem):
-    pairs = [(units, units_v), (d_out, d_out_v), (columns, columns_v), (mixed, mixed_v),
+                  columns_v, d_pre_v, second_v, mixed_v, d_trunk_v, back_v,
+                  first_v, gate_v, in_sem, out_sem, tile_sem, wide_sem):
+    pairs = [(columns, columns_v), (second, second_v), (mixed, mixed_v),
              (d_trunk, d_trunk_v), (back, back_v)]
     steps = d_pre.shape[0]
 
@@ -926,19 +929,12 @@
                     (gate_v, d_gate)][k]
         return pltpu.make_async_copy(src, dst, out_sem.at[k])
 
-    for k in range(3):
-        take(k).start()
+    take(0).start()
     for k in range(steps):
         wide(k).start()
-    for k in range(3, len(pairs)):
+    for k in range(1, len(pairs)):
         take(k).start()
     take(0).wait()
-    take(1).wait()
-    second_v[...] = lax.dot_general(
-        units_v[...], d_out_v[...], (((0,), (0,)), ((), ())),
-        preferred_element_type=F32).astype(BF16)
-    give(0).start()
-    take(2).wait()
     for k in range(steps):
         wide(k).wait()
     tile = first_v.shape[1]
@@ -959,11 +955,13 @@
 
         @pl.when(c == 0)
         def _():
+            take(1).wait()
+            give(0).start()
+            take(2).wait()
+            give(1).start()
             take(3).wait()
-            give(1).start()
+            give(2).start()
             take(4).wait()
-            give(2).start()
-            take(5).wait()
             tasks = d_gate.shape[0]
             eye = jnp.where(
                 lax.broadcasted_iota(jnp.int32, (tasks, LANES), 0)
@@ -981,30 +979,28 @@
         store(c).wait()
 
 
-def finish_all(columns, d_pre, units, d_out, mixed, d_trunk, back, tasks):
+def finish_all(columns, d_pre, second, mixed, d_trunk, back, tasks):
     hbm = pl.BlockSpec(memory_space=pltpu.HBM)
     dma = pltpu.SemaphoreType.DMA
     rows, depth = columns.shape
     steps, group, width = d_pre.shape
-    unit, out = units.shape[1], d_out.shape[1]
     tile = 256
-    ins = (columns, d_pre, units, d_out, mixed, d_trunk, back)
+    ins = (columns, d_pre, second, mixed, d_trunk, back)
     return pl.pallas_call(
         finish_kernel,
         out_shape=(
             jax.ShapeDtypeStruct((depth, width), BF16),
-            jax.ShapeDtypeStruct((unit, out), BF16),
+            jax.ShapeDtypeStruct(second.shape, BF16),
             jax.ShapeDtypeStruct(mixed.shape, BF16),
             jax.ShapeDtypeStruct(d_trunk.shape, BF16),
             jax.ShapeDtypeStruct((tasks, back.shape[0]), BF16),
         ),
-        in_specs=[hbm] * 7,
+        in_specs=[hbm] * 6,
         out_specs=(hbm,) * 5,
         scratch_shapes=[pltpu.VMEM(x.shape, x.dtype) for x in ins] + [
             pltpu.VMEM((depth // tile, tile, width), BF16),
-            pltpu.VMEM((unit, out), BF16),
             pltpu.VMEM((tasks, back.shape[0]), BF16),
-            dma((6,)), dma((4,)), dma((depth // tile,)), dma((steps,)),
+            dma((5,)), dma((4,)), dma((depth // tile,)), dma((steps,)),
         ],
         compiler_params=pltpu.CompilerParams(vmem_limit_bytes=VMEM_BYTES),
     )(*ins)
@@ -1013,11 +1009,11 @@
 def on_square(trunk, w_first, w_second, gates, d_mixed):
     first, second, gate_here = w_first[0], w_second[0], gates[0]
     tasks, group = gate_here.shape
-    columns, d_out, d_pre, units, mixed, d_trunk, back = step_all(
+    columns, d_pre, second_sum, mixed, d_trunk, back = step_all(
         trunk, gate_here, d_mixed.reshape(-1, d_mixed.shape[2]), first, second)
     d_first, d_second, mixed, d_trunk, d_gate = finish_all(
-        columns.reshape(-1, columns.shape[3]), d_pre, units.reshape(-1, units.shape[2]),
-        d_out.reshape(-1, d_out.shape[3]), mixed, d_trunk, back.reshape(group, -1), tasks)
+        columns.reshape(-1, columns.shape[3]), d_pre, second_sum, mixed, d_trunk,
+        back.reshape(group, -1), tasks)
     return (mixed.reshape(d_mixed.shape), d_trunk, d_gate[None], d_first[None], d_second[None])
 
 

time: 70 us -> 69.6 us (level)
  no operation moved by 1% of the time
where the time goes in v6:
time: 69.6 us; the launch traced here: 69.5 us
  Pallas kernels  68.8 us (99%)
    pallas_call x1, Pallas kernels, step_all(): pl.pallas_call(functools.partial(step_kernel, n_e, n_d), out_shape=(jax.S...  60.6 us
    pallas_call x1, Pallas kernels, finish_all(): pl.pallas_call(finish_kernel, out_shape=(jax.ShapeDtypeStruct((depth, wid...  8.23 us

profile of v6, /device:TPU:0, one launch (start us, length us, event | category | flops | bytes accessed | tf_op | source)
XLA Modules:
  0.0 69.5 jit_solution(13385070742060426590)
XLA Ops:
  0.6 60.6 %shard_map.92 = (bf16[4,8,24,1024]{3,2,1,0:T(8,128)(2,1)}, bf16[4,192,2048]{2,1,0:T(8,128)(2,1)}, bf16[512,1024]{1,0:T(8,128)(2,1)}, bf16[192,1024]{1,0:T(8,128)...) custom-call(bf16[24,4096]{1,0:T(8,128)(2,1)} %trunk.1, bf16[8,192]{1,0:T(8,128)(2,1)} %bitcast.15, ...), custom_call_target="tpu_custom_call" | custom-call | tf_op jit(solution)/shard_map/pallas_call | solution.py:859
  61.2 8.2 %shard_map.93 = (bf16[1024,2048]{1,0:T(8,128)(2,1)}, bf16[512,1024]{1,0:T(8,128)(2,1)}, bf16[192,1024]{1,0:T(8,128)(2,1)}, bf16[24,4096]{1,0:T(8,128)(2,1)}, bf16[8,192]{1,0:T(8,128)(2,1)}) custom-call(bf16[768,1024]{1,0:T(8,128)(2,1)} %bitcast.12, bf16[4,192,2048]{2,1,0:T(8,128)(2,1)} %get-tuple-element.17.d_pre, ...), custom_call_target="tpu_custom_call" | custom-call | tf_op jit(solution)/shard_map/pallas_call | solution.py:989
